TPU v7x, 32 devices: a whole 2x2x4 slice. The times are simulated.
32 devices in a mesh: seg: 2 (over y), chan: 8 (over z, core), tm: 2 (over x).
Axes of the slice: x: 2, y: 2, z: 4, core: 2. Of those that a mesh axis runs over, the one named last changes fastest.
Arguments:
- traces: bfloat16 [1024, 12288], P(('seg', 'chan'), 'tm'), parts along dimension 0, may hold values from -14 to 14
- filter_taps: float32 [512, 33], P('chan'), may hold values from -1 to 1
- source_counts: int32 [8], replicated, may hold values from 1 to 36, 96 in all
- source_channel: int32 [8, 36], replicated, may hold values from 0 to 63
- block_sources: int32 [8, 12], P('chan'), may hold values from 0 to 95
Outputs:
- stacked: float32 [1024, 12, 1024], P(('seg', 'chan', 'tm')), parts along dimension 0
There are 2 independent parts, one for each index of `seg`. A program takes and returns all parts, laid end to end along the dimension named above; an argument that names none is the same for every part. Nothing has to cross between parts.
Inputs may be any that keep to these rules, and one draw needn't show every extreme that they name: `source_counts`: the entries sum to 96 and the largest is exactly 36. `source_channel`: only the first source_counts[h] entries of row h name virtual sources.
All inputs are finite; a program needn't handle non-finite values.
Results may differ from a plain program's by a relative error of at most 0.0072.
Values may be sent and summed in bfloat16 or wider, within the bound.
No kernel may reach another device: no remote copies, remote signals or barrier semaphores. Data moves between devices by JAX's collectives and lax.ppermute only.
A program may use at most 64 MiB of HBM per device.

v0:
```python
import math

import jax
import jax.numpy as jnp
from jax import lax
from jax.sharding import PartitionSpec as P

TILE = 64
NFFT = 4096
NF = 512
F0 = 8


def from_behind(block, axis, distance):
    devices = range(lax.axis_size(axis))
    route = [(i - distance, i) for i in devices if i - distance in devices]
    return lax.ppermute(block, axis, route)


def transform_table():
    sample_index = jnp.arange(NFFT, dtype=jnp.int32)[:, None]
    frequency = F0 + jnp.arange(NF, dtype=jnp.int32)[None, :]
    phase_index = frequency * sample_index % NFFT
    angles = phase_index.astype(jnp.float32) * jnp.float32(2.0 * math.pi / NFFT)
    cosine = jnp.cos(angles).astype(jnp.bfloat16)
    sine_part = (-jnp.sin(angles)).astype(jnp.bfloat16)
    return jnp.concatenate([cosine, sine_part], axis=1)


def apply_filter(extended, filter_taps):
    tap_count = filter_taps.shape[1]
    length = extended.shape[1] - (tap_count - 1)
    summed = jnp.zeros((extended.shape[0], length), jnp.float32)
    for tap_index in range(tap_count):
        first_sample = tap_count - 1 - tap_index
        summed = (
            summed
            + filter_taps[:, tap_index : tap_index + 1]
            * extended[:, first_sample : first_sample + length]
        )
    return summed.astype(jnp.bfloat16)


def intersecting(filtered, hop_length):
    channel_count = filtered.shape[0]
    pieces = filtered.reshape(channel_count, -1, hop_length)
    return jnp.concatenate([pieces[:, :-1], pieces[:, 1:]], axis=2)


def whiten(spectra):
    half_width = spectra.shape[-1] // 2
    real_part = spectra[..., :half_width]
    imag_part = spectra[..., half_width:]
    powers = real_part * real_part + imag_part * imag_part
    widths = [(0, 0)] * (powers.ndim - 1) + [(2, 2)]
    padded = jnp.pad(powers, widths)
    smooth = (
        padded[..., 0:half_width]
        + padded[..., 1 : half_width + 1]
        + padded[..., 2 : half_width + 2]
        + padded[..., 3 : half_width + 3]
        + padded[..., 4 : half_width + 4]
    ) / 5.0
    mean_power = jnp.mean(powers, axis=-1, keepdims=True)
    scaling = lax.rsqrt(smooth + 0.1 * mean_power + 1e-06)
    return jnp.concatenate([real_part * scaling, imag_part * scaling], axis=-1).astype(jnp.bfloat16)


def correlate(receivers, sources, factor):
    half_width = receivers.shape[-1] // 2
    receiver_real = receivers[..., :half_width]
    receiver_imag = receivers[..., half_width:]
    source_real = sources[..., :half_width]
    source_imag = sources[..., half_width:]
    real_sum = jnp.sum(source_real * receiver_real + source_imag * receiver_imag, axis=-2)
    imag_sum = jnp.sum(source_real * receiver_imag - source_imag * receiver_real, axis=-2)
    return jnp.concatenate([real_sum, imag_sum], axis=-1) * factor


def source_rows(source_counts, source_channel, wanted):
    offsets = jnp.cumsum(source_counts) - source_counts
    home_group = jnp.sum((wanted[..., None] >= offsets).astype(jnp.int32), axis=-1) - 1
    slot_index = wanted - offsets[home_group]
    local_channel = source_channel[home_group, slot_index]
    return (home_group, slot_index, local_channel)


def shards(traces, filter_taps, source_counts, source_channel, block_sources):
    channels_here, samples_here = traces.shape
    tap_count = filter_taps.shape[1]
    hop_length = NFFT // 2
    halo_width = hop_length + tap_count - 1
    tail_samples = from_behind(traces[:, samples_here - halo_width :], "tm", 1)
    extended = jnp.concatenate([tail_samples, traces], axis=1).astype(jnp.float32)
    filtered = apply_filter(extended, filter_taps)
    windows_here = samples_here // hop_length
    windows = intersecting(filtered, hop_length).reshape(channels_here * windows_here, NFFT)
    spectra = jnp.dot(windows, transform_table(), preferred_element_type=jnp.float32)
    whitened = whiten(spectra).reshape(channels_here, windows_here, 2 * NF)
    home_group, slot_index, local_channel = source_rows(
        source_counts, source_channel, block_sources
    )
    slot_count = source_channel.shape[1]
    group_index = lax.axis_index("chan")
    own_slots = source_channel[group_index]
    slot_rows = whitened[own_slots]
    everything = lax.all_gather(slot_rows, "chan", axis=0, tiled=True)
    picked = everything[home_group * slot_count + slot_index]
    time_groups = lax.axis_size("tm")
    factor = 1.0 / (windows_here * time_groups)
    receivers = whitened.astype(jnp.float32)
    tile_of_row = (
        jnp.arange(channels_here // time_groups * lax.axis_size("tm"), dtype=jnp.int32) // TILE
    )
    sources = picked[tile_of_row].astype(jnp.float32)
    return lax.psum_scatter(
        correlate(receivers[:, None], sources, factor), "tm", scatter_dimension=0, tiled=True
    )


def solution(mesh):
    in_specs = (P(("seg", "chan"), "tm"), P("chan", None), P(), P(), P("chan", None))
    out_specs = P(("seg", "chan", "tm"), None, None)
    return jax.shard_map(shards, mesh=mesh, in_specs=in_specs, out_specs=out_specs, check_vma=False)
```

profile of v0, /device:TPU:0, one launch (start us, length us, event | category | flops | bytes accessed | tf_op | source)
XLA Modules:
  0.0 170.6 jit_solution(2282567406715070541)
XLA Ops:
  6.5 0.0 all-gather.3.cloned.1.call-start
  6.5 1.1 slice.239
  7.6 4.9 %collective-permute-start = (bf16[64,2080]{1,0:T(8,128)(2,1)S(1)}, bf16[64,2080]{1,0:T(8,128)(2,1)S(1)}, u32[]{:S(2)}, u32[]{:S(2)}) collective-permute-start(bf16[64,2080]{1,0:T(8,128)(2,1)S(1)} %slice.239), channel_id=1, source_target_pairs={{0,1},{2,3},{4,5},{6,7},{8,9},{10,11},{12,13},{14,15},{16,17},{18,... | collective-permute-start | bytes 798728 | tf_op jit(solution)/shard_map/ppermute | solution.py:17
  12.5 1.0 slice_bitcast_fusion.33
  13.5 0.0 copy-start
  13.5 35.0 %cosine_convert_fusion = (bf16[4096,512]{1,0:T(8,128)(2,1)}, bf16[4096,512]{1,0:T(8,128)(2,1)}) fusion(s32[512]{0:T(512)S(1)} %iota_add_fusion), kind=kLoop, calls=%fused_computation.14 | loop fusion | flops 35651584 | bytes 8390656 | tf_op jit(solution)/shard_map/convert_element_type | solution.py:25
  48.6 0.7 fusion.51
  49.3 1.0 slice_bitcast_fusion.34
  50.3 0.0 collective-permute-done
  50.3 0.0 copy-done
  50.3 0.3 maximum_convert_fusion
  50.6 18.0 %fusion.11 = bf16[64,8192]{1,0:T(8,128)(2,1)S(1)} fusion(f32[64,8224]{1,0:T(8,128)S(1)} %maximum_convert_fusion, f32[64]{0:T(128)S(1)} %get-tuple-element.48, f32[64]{0:T(128)S(1)} %get-tuple-element.49, f32[64]{0:T(128)S(1)} %get-tuple-element.18, f32[64]{0:T(128)S(1)} %get-tuple-element.19, f32[64]{0:T(128)S(1)} %get-tuple-element.20, ...), kind=kLoop, calls=%fused_computation.23 | loop fusion | flops 34603008 | bytes 70263040 | tf_op jit(solution)/shard_map/convert_element_type | solution.py:41
  68.5 0.8 reshape.253
  69.4 1.3 fusion.58
  70.6 1.5 pad_maximum_fusion
  72.1 2.5 %reshape.254 = bf16[192,4096]{1,0:T(8,128)(2,1)} reshape(bf16[64,3,4096]{2,1,0:T(4,128)(2,1)S(1)} %pad_maximum_fusion) | data formatting | bytes 3145728 | tf_op jit(solution)/shard_map/reshape | solution.py:97
  74.6 5.7 %fusion.3 = f32[192,1024]{1,0:T(8,128)S(1)} fusion(bf16[192,4096]{1,0:T(8,128)(2,1)} %reshape.254, bf16[4096,512]{1,0:T(8,128)(2,1)} %get-tuple-element.51, bf16[4096,512]{1,0:T(8,128)(2,1)} %get-tuple-element.50), kind=kOutput, calls=%fused_computation.9 | convolution fusion | flops 1627389952 | bytes 10747904 | tf_op jit(solution)/shard_map/dot_general | solution.py:98
  80.3 0.1 fusion.57
  80.5 0.5 multiply_convert_fusion.1
  81.0 0.0 copy-start.2
  81.0 0.0 copy-start.1
  81.0 0.1 multiply_convert_fusion
  81.1 0.1 concatenate.39
  81.2 0.1 concatenate.38
  81.3 0.2 pad_maximum_fusion.1
  81.5 1.6 gather_fusion
  83.1 0.0 all-gather.3.cloned.1.call-update
  83.1 0.0 reduce-scatter.2.cloned.1.call-start
  83.2 0.0 copy-done.2
  83.2 0.2 reduce-window.9
  83.4 0.0 copy-done.1
  83.4 0.1 convert_reduce_fusion
  83.5 0.7 gather_fusion.1
  84.2 0.1 concatenate.42
  84.3 0.1 concatenate.41
  84.4 0.3 maximum_convert_fusion.1
  84.7 0.2 slice_bitcast_fusion.1
  84.9 0.1 copy.6
  85.1 0.1 copy.7
  85.2 29.9 %all-gather.3.cloned.1.call-done = bf16[288,3,1024]{2,1,0:T(4,128)(2,1)} async-done(((bf16[36,3,1024]{2,1,0:T(4,128)(2,1)}), bf16[288,3,1024]{2,1,0:T(4,128)(2,1)}) %all-gather.3.cloned.1.call-update) | async-done | bytes 1769488 | tf_op jit(solution)/shard_map/all_gather | solution.py:107
  115.1 2.3 %gather_fusion.2 = bf16[12,3,1024]{2,1,0:T(4,128)(2,1)S(1)} fusion(bf16[288,3,1024]{2,1,0:T(4,128)(2,1)} %all-gather.3.cloned.1.call-done, s32[1024]{0:T(1024)S(1)} %pad_clamp_fusion), kind=kCustom, calls=%fused_computation.2 | custom fusion | bytes 147504 | tf_op jit(solution)/shard_map/gather | solution.py:108
  117.4 1.5 add_reduce_fusion
  118.9 2.1 %maximum_multiply_fusion = f32[64,12,1024]{2,0,1:T(8,128)} fusion(f32[64,12,512]{2,0,1:T(8,128)S(1)} %get-tuple-element.6, f32[64,12,512]{2,0,1:T(8,128)S(1)} %get-tuple-element.5), kind=kLoop, calls=%fused_computation.20 | loop fusion | flops 1572864 | bytes 6291456 | tf_op jit(solution)/shard_map/mul | solution.py:77
  120.9 0.0 reduce-scatter.2.cloned.1.call-update
  121.0 42.8 %reduce-scatter.2.cloned.1.call-done = f32[32,12,1024]{2,0,1:T(8,128)} async-done(((f32[64,12,1024]{2,0,1:T(8,128)}), f32[32,12,1024]{2,0,1:T(8,128)}) %reduce-scatter.2.cloned.1.call-update) | async-done | bytes 1572880 | tf_op jit(solution)/shard_map/reduce_scatter | solution.py:116
  (9 shorter events, 0.1 us)
Async XLA Ops:
  6.5 108.5 %all-gather.3.cloned.1.call-start = ((), (), s32[]{:S(2)}) async-start(), calls=%async_computation.2 | async-start | bytes 2654208 | tf_op jit(solution)/shard_map/all_gather | solution.py:107
  7.6 42.6 %collective-permute-start = (bf16[64,2080]{1,0:T(8,128)(2,1)S(1)}, bf16[64,2080]{1,0:T(8,128)(2,1)S(1)}, u32[]{:S(2)}, u32[]{:S(2)}) collective-permute-start(bf16[64,2080]{1,0:T(8,128)(2,1)S(1)} %slice.239), channel_id=1, source_target_pairs={{0,1},{2,3},{4,5},{6,7},{8,9},{10,11},{12,13},{14,15},{16,17},{18,... | collective-permute-start | bytes 798728 | tf_op jit(solution)/shard_map/ppermute | solution.py:17
  13.5 36.8 %copy-start = (bf16[64,6144]{1,0:T(8,128)(2,1)S(1)}, bf16[64,6144]{1,0:T(8,128)(2,1)}, u32[]{:S(2)}) copy-start(bf16[64,6144]{1,0:T(8,128)(2,1)} %param.5) | copy-start | bytes 2359300
  81.0 2.2 %copy-start.2 = (s32[8]{0:T(128)S(1)}, s32[8]{0:T(128)}, u32[]{:S(2)}) copy-start(s32[8]{0:T(128)} %param.7) | copy-start | bytes 100
  81.0 2.4 %copy-start.1 = (s32[1,12]{1,0:T(1,128)S(1)}, s32[1,12]{1,0:T(1,128)}, u32[]{:S(2)}) copy-start(s32[1,12]{1,0:T(1,128)} %param.9) | copy-start | bytes 148
  83.1 80.7 %reduce-scatter.2.cloned.1.call-start = ((), (), s32[]{:S(2)}) async-start(), calls=%async_computation.1 | async-start | bytes 4718592 | tf_op jit(solution)/shard_map/reduce_scatter | solution.py:116
Sparse Core Ops, SparseCore 0:
  83.3 31.7 all-gather.2
  121.1 42.6 reduce-scatter.1
where the time goes:
time: 171 us
  waiting for transfers between devices  72.8 us (43%)
  other arithmetic  60.5 us (35%)
  between operations  13.6 us (8%)
  local copies, waits for them, and re-layouts  13.1 us (8%)
  matrix products  5.69 us (3%)
  starting transfers between devices  4.93 us (3%)
    reduce_scatter x1, waiting for transfers between devices, shards(): lax.psum_scatter(correlate(receivers[:, None], sources, factor), 'tm', sc...  42.8 us
    convert_element_type x1, other arithmetic, transform_table(): cosine = jnp.cos(angles).astype(jnp.bfloat16)  35 us
    all_gather x1, waiting for transfers between devices, shards(): everything = lax.all_gather(slot_rows, 'chan', axis=0, tiled=True)  29.9 us
    convert_element_type x1, other arithmetic, apply_filter(): return summed.astype(jnp.bfloat16)  18 us
    dot_general x1, matrix products, shards(): jnp.dot(windows, transform_table(), preferred_element_type=jnp.float32)  5.69 us
    ppermute x1, starting transfers between devices, from_behind(): return lax.ppermute(block, axis, route)  4.89 us
  transfers between devices with their start and end apart: 3, of which 2 were waited for; matrix products, arithmetic and copies ran while one was open for 23% of the time, Pallas kernels for 0%

commit v1 on v0

v1 whole, which is shorter than its diff:
```python
import functools

import jax
import jax.numpy as jnp
import numpy as np
from jax import lax
from jax.experimental import pallas as pl
from jax.experimental.pallas import tpu as pltpu
from jax.sharding import PartitionSpec as P

NFFT = 4096
NF = 512
F0 = 8
STEP = 32
F32 = jnp.float32
BF16 = jnp.bfloat16


def angle_factors():
    bins = F0 + np.arange(NF)
    row = np.arange(STEP)[:, None]
    coarse = (bins * row * STEP % NFFT) * (2.0 * np.pi / NFFT)
    fine = (bins * row % NFFT) * (2.0 * np.pi / NFFT)
    parts = [np.cos(coarse), np.sin(coarse), np.cos(fine), np.sin(fine)]
    return np.stack(parts).astype(np.float32)


def split_two(x):
    high = x.astype(BF16)
    low = (x - high.astype(F32)).astype(BF16)
    return high, low


def dot(a, b):
    return jnp.dot(a, b, preferred_element_type=F32)


def dot_three(x, table_high, table_low):
    high, low = split_two(x)
    return dot(high, table_high) + dot(low, table_high) + dot(high, table_low)


def spectra_kernel(
    shape,
    where,
    counts,
    slots,
    *refs,
):
    channels, windows, tap_count, pairs, block_rows, chips, times = shape
    wanted = refs[:chips]
    traces, halo, taps, factors = refs[chips : chips + 4]
    keep, send = refs[chips + 4 : chips + 6]
    blocks = refs[chips + 6 : chips + 6 + times]
    high, low, chosen, spectra, white = refs[chips + 6 + times :]
    quarter = NFFT // 4
    half = NFFT // 2

    def make_table(a, carry):
        cos_a = factors[0, pl.ds(a, 1), :]
        sin_a = factors[1, pl.ds(a, 1), :]
        cos_b = factors[2]
        sin_b = factors[3]
        rows = pl.ds(pl.multiple_of(a * STEP, STEP), STEP)
        h, l = split_two(cos_a * cos_b - sin_a * sin_b)
        high[rows, :NF] = h
        low[rows, :NF] = l
        h, l = split_two(-(sin_a * cos_b + cos_a * sin_b))
        high[rows, NF:] = h
        low[rows, NF:] = l
        return carry

    lax.fori_loop(0, quarter // STEP, make_table, 0)

    group = where[0]
    first = jnp.int32(0)
    for g in range(counts.shape[0]):
        first = first + jnp.where(g < group, counts[g], 0)
    owned = counts[group]
    width = windows * channels
    column = lax.broadcasted_iota(jnp.int32, (1, width), 1)
    base = 2 * chips * block_rows
    chosen[:base, :] = jnp.zeros((base, width), F32)
    for core in range(2):
        for d in range(chips):
            for p in range(pairs):
                slot = wanted[d][core, p] - first
                mine = (slot >= 0) & (slot < owned)
                channel = slots[group, jnp.where(mine, slot, 0)]
                at = jnp.where(mine, channel, -width)
                row = (core * chips + d) * block_rows + p
                for w in range(windows):
                    r = row + w * pairs
                    chosen[r : r + 1, :] = (column == at + w * channels).astype(F32)
    part = channels // times
    for d in range(times):
        start = (where[1] ^ d) * part
        for w in range(windows):
            r = base + (d * windows + w) * part
            line = lax.broadcasted_iota(jnp.int32, (part, width), 0)
            col = lax.broadcasted_iota(jnp.int32, (part, width), 1)
            chosen[r : r + part, :] = (col == line + start + w * channels).astype(F32)

    filter_taps = taps[...]
    h, l = split_two(filter_taps)
    t_rows = high[:tap_count, :]
    response = dot(h, t_rows) + dot(l, t_rows) + dot(h, low[:tap_count, :])
    lag = tap_count - 1
    tile = halo.shape[1] - half
    ends = [halo[:, :tile], halo[:, half : half + tile]]
    for b in range(1, windows + 1):
        ends.append(traces[:, b * half - tile : b * half])
    lane = lax.broadcasted_iota(jnp.int32, (channels, tile), 1)
    edges = []
    for w in range(windows):
        apart = ends[w].astype(F32) - ends[w + 2].astype(F32)
        total = jnp.zeros((channels, tile), F32)
        for k in range(1, tap_count):
            turned = pltpu.roll(apart, k, 1)
            total = total + filter_taps[:, k : k + 1] * jnp.where(lane < k, turned, 0.0)
        edges.append(total[:, :lag])
    edge = dot_three(jnp.concatenate(edges, axis=0), high[:lag, :], low[:lag, :])
    spectra[...] = edge

    samples = [halo[:, tile : tile + quarter], halo[:, tile + quarter :]]
    for q in range(traces.shape[1] // quarter):
        samples.append(traces[:, q * quarter : (q + 1) * quarter])
    x = jnp.concatenate(samples, axis=0)
    chunk = 256
    turn = lax.broadcasted_iota(jnp.int32, (1, chunk), 1) % 4
    odd = (turn % 2) == 1
    sign = jnp.where(odd, -1.0, 1.0)
    sign_r = jnp.where(turn < 2, 1.0, -1.0)
    sign_i = jnp.where((turn == 0) | (turn == 3), 1.0, -1.0)
    for f in range(0, NF, chunk):
        re = slice(f, f + chunk)
        im = slice(NF + f, NF + f + chunk)
        dr = dot(x, high[:, re]) + dot(x, low[:, re])
        di = dot(x, high[:, im]) + dot(x, low[:, im])
        hr, hi = [], []
        for b in range(windows + 1):
            even_rows = slice(2 * b * channels, (2 * b + 1) * channels)
            odd_rows = slice((2 * b + 1) * channels, (2 * b + 2) * channels)
            br, bi = dr[odd_rows], di[odd_rows]
            hr.append(dr[even_rows] + sign_r * jnp.where(odd, bi, br))
            hi.append(di[even_rows] + sign_i * jnp.where(odd, br, bi))
        pr, pi = response[:, re], response[:, im]
        for w in range(windows):
            rows = slice(w * channels, (w + 1) * channels)
            xr = hr[w] + sign * hr[w + 1]
            xi = hi[w] + sign * hi[w + 1]
            spectra[rows, re] = spectra[rows, re] + (xr * pr - xi * pi)
            spectra[rows, im] = spectra[rows, im] + (xr * pi + xi * pr)

    rows_at_once = 16
    place = lax.broadcasted_iota(jnp.int32, (rows_at_once, NF), 1)

    def whiten(i, carry):
        rows = pl.ds(pl.multiple_of(i * rows_at_once, rows_at_once), rows_at_once)
        re = spectra[rows, :NF]
        im = spectra[rows, NF:]
        power = re * re + im * im
        smooth = power
        for s in (1, 2):
            smooth = smooth + jnp.where(place >= s, pltpu.roll(power, s, 1), 0.0)
            smooth = smooth + jnp.where(place < NF - s, pltpu.roll(power, NF - s, 1), 0.0)
        mean = jnp.mean(power, axis=1, keepdims=True)
        scaling = lax.rsqrt(smooth / 5.0 + 0.1 * mean + 1e-06)
        white[rows, :NF] = (re * scaling).astype(BF16)
        white[rows, NF:] = (im * scaling).astype(BF16)
        return carry

    lax.fori_loop(0, width // rows_at_once, whiten, 0)

    picks = chosen[...].astype(BF16)
    for f in range(0, 2 * NF, chunk):
        cols = slice(f, f + chunk)
        out = dot(picks, white[:, cols]).astype(BF16)
        keep[:, cols] = out[: base // 2]
        send[:, cols] = out[base // 2 : base]
        for d in range(times):
            r = base + d * windows * part
            blocks[d][:, cols] = out[r : r + windows * part]


def correlate_kernel(windows, pairs, factor, *refs):
    count = (len(refs) - 2) // 2
    receivers = refs[:count]
    sources = refs[count : 2 * count]
    out = refs[2 * count]
    held = refs[2 * count + 1]

    @pl.when(pl.program_id(0) == 0)
    def _():
        for d in range(count):
            for w in range(windows):
                rows = sources[d][w * pairs : (w + 1) * pairs, :]
                held[d * windows + w, :pairs, :] = rows.astype(F32) * factor

    for c in range(out.shape[0]):
        for f in range(0, NF, 128):
            re = slice(f, f + 128)
            im = slice(NF + f, NF + f + 128)
            total_r = jnp.zeros((pairs, 128), F32)
            total_i = jnp.zeros((pairs, 128), F32)
            for d in range(count):
                for w in range(windows):
                    rr = receivers[d][w, c : c + 1, re].astype(F32)
                    ri = receivers[d][w, c : c + 1, im].astype(F32)
                    sr = held[d * windows + w, :pairs, re]
                    si = held[d * windows + w, :pairs, im]
                    total_r = total_r + (sr * rr + si * ri)
                    total_i = total_i + (sr * ri - si * rr)
            out[c, :, re] = total_r
            out[c, :, im] = total_i


def shards(traces, filter_taps, source_counts, source_channel, block_sources):
    channels, samples = traces.shape
    tap_count = filter_taps.shape[1]
    pairs = block_sources.shape[1]
    half = NFFT // 2
    windows = samples // half
    groups = lax.axis_size("chan")
    times = lax.axis_size("tm")
    chips = groups // 2
    part = channels // times
    block_rows = -(-windows * pairs // 8) * 8

    def across(x, axis, distance):
        size = lax.axis_size(axis)
        return lax.ppermute(x, axis, [(i, i ^ distance) for i in range(size)])

    tail = traces[:, samples - half - 128 :]
    halo = lax.ppermute(tail, "tm", [(i - 1, i) for i in range(1, times)])
    both = jnp.concatenate([block_sources, across(block_sources, "chan", 1)], axis=0)
    wanted = [both] + [across(both, "chan", 2 * d) for d in range(1, chips)]
    where = jnp.stack([lax.axis_index("chan"), lax.axis_index("tm")]).astype(jnp.int32)

    shape = (channels, windows, tap_count, pairs, block_rows, chips, times)
    smem = pl.BlockSpec(memory_space=pltpu.SMEM)
    vmem = pl.BlockSpec(memory_space=pltpu.VMEM)
    width = windows * channels
    all_rows = 2 * chips * block_rows + width
    outs = pl.pallas_call(
        functools.partial(spectra_kernel, shape),
        out_shape=[jax.ShapeDtypeStruct((chips * block_rows, 2 * NF), BF16)] * 2
        + [jax.ShapeDtypeStruct((windows * part, 2 * NF), BF16)] * times,
        in_specs=[smem] * (3 + chips) + [vmem] * 4,
        out_specs=[vmem] * (2 + times),
        scratch_shapes=[
            pltpu.VMEM((NFFT // 4, 2 * NF), BF16),
            pltpu.VMEM((NFFT // 4, 2 * NF), BF16),
            pltpu.VMEM((all_rows, width), F32),
            pltpu.VMEM((width, 2 * NF), F32),
            pltpu.VMEM((width, 2 * NF), BF16),
        ],
        name="spectra",
    )(
        where,
        source_counts,
        source_channel,
        *wanted,
        traces,
        halo,
        filter_taps,
        jnp.asarray(angle_factors()),
    )
    keep, send, blocks = outs[0], outs[1], outs[2:]
    gathered = keep + across(send, "chan", 1)
    pieces = [gathered[d * block_rows : (d + 1) * block_rows] for d in range(chips)]
    mine = pieces[0]
    for d in range(1, chips):
        mine = mine + across(pieces[d], "chan", 2 * d)
    receivers = [blocks[0]] + [across(blocks[d], "tm", d) for d in range(1, times)]
    receivers = [r.reshape(windows, part, 2 * NF) for r in receivers]
    sources = [mine] + [across(mine, "tm", d) for d in range(1, times)]

    step = 8
    factor = 1.0 / (windows * times)
    return pl.pallas_call(
        functools.partial(correlate_kernel, windows, pairs, factor),
        out_shape=jax.ShapeDtypeStruct((part, pairs, 2 * NF), F32),
        grid=(part // step,),
        in_specs=[pl.BlockSpec((windows, step, 2 * NF), lambda i: (0, i, 0))] * times
        + [pl.BlockSpec((block_rows, 2 * NF), lambda i: (0, 0))] * times,
        out_specs=pl.BlockSpec((step, pairs, 2 * NF), lambda i: (i, 0, 0)),
        scratch_shapes=[pltpu.VMEM((windows * times, -(-pairs // 8) * 8, 2 * NF), F32)],
        name="correlate",
    )(*receivers, *sources)


def solution(mesh):
    in_specs = (P(("seg", "chan"), "tm"), P("chan", None), P(), P(), P("chan", None))
    out_specs = P(("seg", "chan", "tm"), None, None)
    return jax.shard_map(shards, mesh=mesh, in_specs=in_specs, out_specs=out_specs, check_vma=False)
```

time: 171 us -> 55.9 us (0.33)
  other arithmetic: 60.5 us -> 2.33 us
  waiting for transfers between devices: 72.8 us -> 17.6 us
  Pallas kernels: 0 us -> 14.3 us
  between operations: 13.6 us -> 0.12 us
  starting transfers between devices: 4.93 us -> 13 us
  matrix products: 5.69 us -> 0 us
  local copies, waits for them, and re-layouts: 13.1 us -> 7.95 us
    convert_element_type x4 -> x0, other arithmetic: 53.6 us -> none  [the longest x1 35 us: transform_table(): cosine = jnp.cos(angles).astype(jnp.bfloat16)]
    reduce_scatter x1 -> x0, waiting for transfers between devices: 42.8 us -> none  [shards(): lax.psum_scatter(correlate(receivers[:, None], sources, factor), 'tm', sc...]
    all_gather x1 -> x0, waiting for transfers between devices: 29.9 us -> none  [shards(): everything = lax.all_gather(slot_rows, 'chan', axis=0, tiled=True)]
    ppermute x1 -> x11, waiting for transfers between devices: 0.01 us -> 17.6 us  [the longest x10 17.6 us: across(): return lax.ppermute(x, axis, [(i, i ^ distance) for i in range(size)])]
    pallas_call x0 -> x2, Pallas kernels: none -> 14.3 us  [the longest x1 9.86 us: shards(): pl.pallas_call(functools.partial(spectra_kernel, shape), out_shape=[jax.S...]
    ppermute x1 -> x11, starting transfers between devices: 4.89 us -> 13 us  [the longest x10 8.14 us: across(): return lax.ppermute(x, axis, [(i, i ^ distance) for i in range(size)])]
    dot_general x1 -> x0, matrix products: 5.69 us -> none  [shards(): jnp.dot(windows, transform_table(), preferred_element_type=jnp.float32)]
    gather x3 -> x0, local copies, waits for them, and re-layouts: 4.52 us -> none  [the longest x1 2.29 us: shards(): picked = everything[home_group * slot_count + slot_index]]
  transfers between devices with their start and end apart: 3 -> 11, of which waited for: 2 -> 7; matrix products, arithmetic and copies ran while one was open for 23% -> 5% of each run, Pallas kernels for 0% -> 0%
where the time goes in v1:
time: 55.9 us; the launch traced here: 55.4 us
  waiting for transfers between devices  17.6 us (31%)
  Pallas kernels  14.3 us (26%)
  starting transfers between devices  13 us (23%)
  local copies, waits for them, and re-layouts  7.95 us (14%)
  other arithmetic  2.33 us (4%)
    ppermute x10, waiting for transfers between devices, across(): return lax.ppermute(x, axis, [(i, i ^ distance) for i in range(size)])  17.6 us
    pallas_call x1, Pallas kernels, shards(): pl.pallas_call(functools.partial(spectra_kernel, shape), out_shape=[jax.S...  9.86 us
    ppermute x10, starting transfers between devices, across(): return lax.ppermute(x, axis, [(i, i ^ distance) for i in range(size)])  8.14 us
    ppermute x1, starting transfers between devices, shards(): halo = lax.ppermute(tail, 'tm', [(i - 1, i) for i in range(1, times)])  4.89 us
    pallas_call x1, Pallas kernels, shards(): pl.pallas_call(functools.partial(correlate_kernel, windows, pairs, factor...  4.47 us
    pallas_call x1, local copies, waits for them, and re-layouts, shards(): pl.pallas_call(functools.partial(correlate_kernel, windows, pairs, factor...  3.65 us
    unnamed x17, local copies, waits for them, and re-layouts  3.31 us
  transfers between devices with their start and end apart: 11, of which 7 were waited for; matrix products, arithmetic and copies ran while one was open for 5% of the time, Pallas kernels for 0%

profile of v1, /device:TPU:0, one launch (start us, length us, event | category | flops | bytes accessed | tf_op | source)
XLA Modules:
  0.0 55.4 jit_solution(17852312792474935647)
XLA Ops:
  0.0 1.0 %slice.15 = bf16[64,2176]{1,0:T(8,128)(2,1)S(1)} slice(bf16[64,6144]{1,0:T(8,128)(2,1)} %refs_4_.1), slice={[0:64], [3968:6144]} | slice | bytes 557056 | tf_op jit(solution)/shard_map/slice | solution.py:234
  1.0 4.9 %collective-permute-start.4 = (bf16[64,2176]{1,0:T(8,128)(2,1)S(1)}, bf16[64,2176]{1,0:T(8,128)(2,1)S(1)}, u32[]{:S(2)}, u32[]{:S(2)}) collective-permute-start(bf16[64,2176]{1,0:T(8,128)(2,1)S(1)} %slice.15), channel_id=1, source_target_pairs={{0,1},{2,3},{4,5},{6,7},{8,9},{10,11},{12,13},{14,15},{16,17},{18,... | collective-permute-start | bytes 835592 | tf_op jit(solution)/shard_map/ppermute | solution.py:235
  5.9 0.1 collective-permute-start
  6.0 1.4 %copy.7.refs_6_ = f32[64,33]{1,0:T(8,128)} copy(f32[64,33]{0,1:T(8,128)} %param.7) | data formatting | bytes 16896 | tf_op args[1]
  7.4 0.6 %pad_add_fusion.1.where = s32[2]{0:T(128)} fusion(s32[1]{0:T(128)} %bitcast.1, s32[1]{0:T(128)} %bitcast), kind=kLoop, calls=%fused_computation.4 | loop fusion | flops 2 | bytes 16 | tf_op jit(solution)/shard_map/stack | solution.py:238
  8.0 0.0 collective-permute-done
  8.0 0.7 %pad_add_fusion.refs_0_ = s32[2,12]{1,0:T(2,128)S(1)} fusion(s32[1,12]{1,0:T(1,128)S(1)} %collective-permute-done, s32[1,12]{1,0:T(1,128)} %param.10), kind=kLoop, calls=%fused_computation.3 | loop fusion | flops 24 | bytes 192 | tf_op jit(solution)/shard_map/concatenate | solution.py:236
  8.6 0.0 copy-start.4
  8.6 3.7 %collective-permute-start.3 = (s32[2,12]{1,0:T(2,128)S(1)}, s32[2,12]{1,0:T(2,128)S(1)}, u32[]{:S(2)}, u32[]{:S(2)}) collective-permute-start(s32[2,12]{1,0:T(2,128)S(1)} %pad_add_fusion.refs_0_), channel_id=1, source_target_pairs={{0,12},{2,14},{4,8},{6,10},{8,4},{10,6},{12,0},{14,2},{1,13},{3,15... | collective-permute-start | bytes 296 | tf_op jit(solution)/shard_map/ppermute | solution.py:232
  12.3 0.0 collective-permute-start.2
  12.3 0.8 %collective-permute-start.1 = (s32[2,12]{1,0:T(2,128)S(1)}, s32[2,12]{1,0:T(2,128)S(1)}, u32[]{:S(2)}, u32[]{:S(2)}) collective-permute-start(s32[2,12]{1,0:T(2,128)S(1)} %pad_add_fusion.refs_0_), channel_id=1, source_target_pairs={{0,4},{2,6},{4,0},{6,2},{8,12},{10,14},{12,8},{14,10},{1,5},{3,7},... | collective-permute-start | bytes 296 | tf_op jit(solution)/shard_map/ppermute | solution.py:232
  13.1 1.0 %collective-permute-done.3.refs_3_ = s32[2,12]{1,0:T(2,128)S(1)} collective-permute-done((s32[2,12]{1,0:T(2,128)S(1)}, s32[2,12]{1,0:T(2,128)S(1)}, u32[]{:S(2)}, u32[]{:S(2)}) %collective-permute-start.3) | collective-permute-done | bytes 128 | tf_op jit(solution)/shard_map/ppermute | solution.py:232
  14.1 0.0 copy-start.5
  14.1 2.7 %collective-permute-done.2.refs_2_ = s32[2,12]{1,0:T(2,128)S(1)} collective-permute-done((s32[2,12]{1,0:T(2,128)S(1)}, s32[2,12]{1,0:T(2,128)S(1)}, u32[]{:S(2)}, u32[]{:S(2)}) %collective-permute-start.2) | collective-permute-done | bytes 128 | tf_op jit(solution)/shard_map/ppermute | solution.py:232
  16.8 0.0 copy-start.6
  16.8 0.0 collective-permute-done.1.refs_1_
  16.8 0.0 copy-start.7
  16.8 0.0 collective-permute-done.4.refs_5_
  16.8 0.0 copy-done.4
  16.8 0.0 copy-done.5
  16.8 0.5 copy-done.6
  17.3 0.0 copy-done.7
  17.3 0.0 copy-start.1
  17.3 0.7 %copy-done.1 = bf16[64,2176]{1,0:T(8,128)(2,1)} copy-done((bf16[64,2176]{1,0:T(8,128)(2,1)}, bf16[64,2176]{1,0:T(8,128)(2,1)S(1)}, u32[]{:S(2)}) %copy-start.1) | copy-done | bytes 278552
  18.0 9.9 %spectra.1 = (bf16[160,1024]{1,0:T(8,128)(2,1)}, bf16[160,1024]{1,0:T(8,128)(2,1)}, bf16[96,1024]{1,0:T(8,128)(2,1)}, bf16[96,1024]{1,0:T(8,128)(2,1)}) custom-call(s32[2]{0:T(128)} %pad_add_fusion.1.where, s32[8]{0:T(128)} %counts.1, s32[8,36]{1,0:T(8,128)} %slots.1, s32[2,12]{1,0:T(2,128)} %copy-done.4, s32[2,12]{1,0:T(2,128)} %copy-done.7, ...), custom_call_target="tpu_custom_call" | custom-call | tf_op jit(solution)/shard_map/spectra/pallas_call | solution.py:245
  27.9 0.0 collective-permute-start.6
  27.9 1.8 %collective-permute-done.6 = bf16[160,1024]{1,0:T(8,128)(2,1)S(1)} collective-permute-done((bf16[160,1024]{1,0:T(8,128)(2,1)}, bf16[160,1024]{1,0:T(8,128)(2,1)S(1)}, u32[]{:S(2)}, u32[]{:S(2)}) %collective-permute-start.6) | collective-permute-done | bytes 327712 | tf_op jit(solution)/shard_map/ppermute | solution.py:232
  29.7 1.1 %add.12 = bf16[160,1024]{1,0:T(8,128)(2,1)S(1)} add(bf16[160,1024]{1,0:T(8,128)(2,1)} %get-tuple-element.11, bf16[160,1024]{1,0:T(8,128)(2,1)S(1)} %collective-permute-done.6) | non-fusion elementwise | flops 163840 | bytes 983040 | tf_op jit(solution)/shard_map/add | solution.py:270
  30.8 0.1 collective-permute-start.7
  30.9 3.5 %collective-permute-start.9 = (bf16[40,1024]{1,0:T(8,128)(2,1)S(1)}, bf16[40,1024]{1,0:T(8,128)(2,1)S(1)}, u32[]{:S(2)}, u32[]{:S(2)}) collective-permute-start(bf16[40,1024]{1,0:T(8,128)(2,1)S(1)} %get-tuple-element.14), channel_id=1, source_target_pairs={{0,12},{2,14},{4,8},{6,10},{8,4},{10,6},{12,0},{14,2},{1,13},{3,15... | collective-permute-start | bytes 245768 | tf_op jit(solution)/shard_map/ppermute | solution.py:232
  34.4 0.0 collective-permute-start.8
  34.4 0.0 collective-permute-start.5
  34.4 1.0 %collective-permute-done.7 = bf16[40,1024]{1,0:T(8,128)(2,1)S(1)} collective-permute-done((bf16[40,1024]{1,0:T(8,128)(2,1)S(1)}, bf16[40,1024]{1,0:T(8,128)(2,1)S(1)}, u32[]{:S(2)}, u32[]{:S(2)}) %collective-permute-start.7) | collective-permute-done | bytes 81952 | tf_op jit(solution)/shard_map/ppermute | solution.py:232
  35.4 4.1 %collective-permute-done.9 = bf16[40,1024]{1,0:T(8,128)(2,1)S(1)} collective-permute-done((bf16[40,1024]{1,0:T(8,128)(2,1)S(1)}, bf16[40,1024]{1,0:T(8,128)(2,1)S(1)}, u32[]{:S(2)}, u32[]{:S(2)}) %collective-permute-start.9) | collective-permute-done | bytes 81952 | tf_op jit(solution)/shard_map/ppermute | solution.py:232
  39.5 2.5 %collective-permute-done.8 = bf16[40,1024]{1,0:T(8,128)(2,1)S(1)} collective-permute-done((bf16[40,1024]{1,0:T(8,128)(2,1)S(1)}, bf16[40,1024]{1,0:T(8,128)(2,1)S(1)}, u32[]{:S(2)}, u32[]{:S(2)}) %collective-permute-start.8) | collective-permute-done | bytes 81952 | tf_op jit(solution)/shard_map/ppermute | solution.py:232
  42.1 0.0 copy-start
  42.1 0.1 collective-permute-start.10
  42.2 0.0 collective-permute-done.5
  42.2 0.0 copy-start.2
  42.2 4.4 %collective-permute-done.10.refs_3_ = bf16[40,1024]{1,0:T(8,128)(2,1)S(1)} collective-permute-done((bf16[40,1024]{1,0:T(8,128)(2,1)S(1)}, bf16[40,1024]{1,0:T(8,128)(2,1)S(1)}, u32[]{:S(2)}, u32[]{:S(2)}) %collective-permute-start.10) | collective-permute-done | bytes 81952 | tf_op jit(solution)/shard_map/ppermute | solution.py:232
  46.6 0.0 copy-start.3
  46.6 0.0 copy-done
  46.6 0.0 copy-done.2
  46.6 0.6 %copy-done.3 = bf16[40,1024]{1,0:T(8,128)(2,1)} copy-done((bf16[40,1024]{1,0:T(8,128)(2,1)}, bf16[40,1024]{1,0:T(8,128)(2,1)S(1)}, u32[]{:S(2)}) %copy-start.3) | copy-done | bytes 81944
  47.3 4.5 %correlate.1 = f32[32,12,1024]{2,1,0:T(8,128)} custom-call(bf16[3,32,1024]{2,1,0:T(8,128)(2,1)} %bitcast.4, bf16[3,32,1024]{2,1,0:T(8,128)(2,1)} %bitcast.5, bf16[40,1024]{1,0:T(8,128)(2,1)} %copy-done, bf16[40,1024]{1,0:T(8,128)(2,1)} %copy-done.3), custom_call_target="tpu_custom_call" | custom-call | tf_op jit(solution)/shard_map/correlate/pallas_call | solution.py:281
  51.7 3.6 %copy.8 = f32[32,12,1024]{2,0,1:T(8,128)} copy(f32[32,12,1024]{2,1,0:T(8,128)} %correlate.1) | data formatting | bytes 3145728 | tf_op jit(solution)/shard_map/correlate/pallas_call | solution.py:281
  (2 shorter events, 0.0 us)
Async XLA Ops:
  1.0 15.8 %collective-permute-start.4 = (bf16[64,2176]{1,0:T(8,128)(2,1)S(1)}, bf16[64,2176]{1,0:T(8,128)(2,1)S(1)}, u32[]{:S(2)}, u32[]{:S(2)}) collective-permute-start(bf16[64,2176]{1,0:T(8,128)(2,1)S(1)} %slice.15), channel_id=1, source_target_pairs={{0,1},{2,3},{4,5},{6,7},{8,9},{10,11},{12,13},{14,15},{16,17},{18,... | collective-permute-start | bytes 835592 | tf_op jit(solution)/shard_map/ppermute | solution.py:235
  5.9 2.1 %collective-permute-start = (s32[1,12]{1,0:T(1,128)}, s32[1,12]{1,0:T(1,128)S(1)}, u32[]{:S(2)}, u32[]{:S(2)}) collective-permute-start(s32[1,12]{1,0:T(1,128)} %param.10), channel_id=1, source_target_pairs={{0,2},{2,0},{4,6},{6,4},{8,10},{10,8},{12,14},{14,12},{1,3},{3,1},... | collective-permute-start | bytes 152 | tf_op jit(solution)/shard_map/ppermute | solution.py:232
  8.6 8.2 %copy-start.4 = (s32[2,12]{1,0:T(2,128)}, s32[2,12]{1,0:T(2,128)S(1)}, u32[]{:S(2)}) copy-start(s32[2,12]{1,0:T(2,128)S(1)} %pad_add_fusion.refs_0_) | copy-start | bytes 292
  8.6 5.4 %collective-permute-start.3 = (s32[2,12]{1,0:T(2,128)S(1)}, s32[2,12]{1,0:T(2,128)S(1)}, u32[]{:S(2)}, u32[]{:S(2)}) collective-permute-start(s32[2,12]{1,0:T(2,128)S(1)} %pad_add_fusion.refs_0_), channel_id=1, source_target_pairs={{0,12},{2,14},{4,8},{6,10},{8,4},{10,6},{12,0},{14,2},{1,13},{3,15... | collective-permute-start | bytes 296 | tf_op jit(solution)/shard_map/ppermute | solution.py:232
  12.3 4.5 %collective-permute-start.2 = (s32[2,12]{1,0:T(2,128)S(1)}, s32[2,12]{1,0:T(2,128)S(1)}, u32[]{:S(2)}, u32[]{:S(2)}) collective-permute-start(s32[2,12]{1,0:T(2,128)S(1)} %pad_add_fusion.refs_0_), channel_id=1, source_target_pairs={{0,8},{2,10},{4,12},{6,14},{8,0},{10,2},{12,4},{14,6},{1,9},{3,11}... | collective-permute-start | bytes 296 | tf_op jit(solution)/shard_map/ppermute | solution.py:232
  12.3 4.5 %collective-permute-start.1 = (s32[2,12]{1,0:T(2,128)S(1)}, s32[2,12]{1,0:T(2,128)S(1)}, u32[]{:S(2)}, u32[]{:S(2)}) collective-permute-start(s32[2,12]{1,0:T(2,128)S(1)} %pad_add_fusion.refs_0_), channel_id=1, source_target_pairs={{0,4},{2,6},{4,0},{6,2},{8,12},{10,14},{12,8},{14,10},{1,5},{3,7},... | collective-permute-start | bytes 296 | tf_op jit(solution)/shard_map/ppermute | solution.py:232
  14.1 2.7 %copy-start.5 = (s32[2,12]{1,0:T(2,128)}, s32[2,12]{1,0:T(2,128)S(1)}, u32[]{:S(2)}) copy-start(s32[2,12]{1,0:T(2,128)S(1)} %collective-permute-done.3.refs_3_) | copy-start | bytes 292
  16.8 0.5 copy-start.6
  16.8 0.6 %copy-start.7 = (s32[2,12]{1,0:T(2,128)}, s32[2,12]{1,0:T(2,128)S(1)}, u32[]{:S(2)}) copy-start(s32[2,12]{1,0:T(2,128)S(1)} %collective-permute-done.1.refs_1_) | copy-start | bytes 292
  17.3 0.7 %copy-start.1 = (bf16[64,2176]{1,0:T(8,128)(2,1)}, bf16[64,2176]{1,0:T(8,128)(2,1)S(1)}, u32[]{:S(2)}) copy-start(bf16[64,2176]{1,0:T(8,128)(2,1)S(1)} %collective-permute-done.4.refs_5_) | copy-start | bytes 835588
  27.9 1.8 %collective-permute-start.6 = (bf16[160,1024]{1,0:T(8,128)(2,1)}, bf16[160,1024]{1,0:T(8,128)(2,1)S(1)}, u32[]{:S(2)}, u32[]{:S(2)}) collective-permute-start(bf16[160,1024]{1,0:T(8,128)(2,1)} %get-tuple-element.12), channel_id=1, source_target_pairs={{0,2},{2,0},{4,6},{6,4},{8,10},{10,8},{12,14},{14,12},{1,3},{3,1},... | collective-permute-start | bytes 983048 | tf_op jit(solution)/shard_map/ppermute | solution.py:232
  30.8 4.6 %collective-permute-start.7 = (bf16[40,1024]{1,0:T(8,128)(2,1)S(1)}, bf16[40,1024]{1,0:T(8,128)(2,1)S(1)}, u32[]{:S(2)}, u32[]{:S(2)}) collective-permute-start(bf16[40,1024]{1,0:T(8,128)(2,1)S(1)} %get-tuple-element.13), channel_id=1, source_target_pairs={{0,4},{2,6},{4,0},{6,2},{8,12},{10,14},{12,8},{14,10},{1,5},{3,7},... | collective-permute-start | bytes 245768 | tf_op jit(solution)/shard_map/ppermute | solution.py:232
  30.9 8.6 %collective-permute-start.9 = (bf16[40,1024]{1,0:T(8,128)(2,1)S(1)}, bf16[40,1024]{1,0:T(8,128)(2,1)S(1)}, u32[]{:S(2)}, u32[]{:S(2)}) collective-permute-start(bf16[40,1024]{1,0:T(8,128)(2,1)S(1)} %get-tuple-element.14), channel_id=1, source_target_pairs={{0,12},{2,14},{4,8},{6,10},{8,4},{10,6},{12,0},{14,2},{1,13},{3,15... | collective-permute-start | bytes 245768 | tf_op jit(solution)/shard_map/ppermute | solution.py:232
  34.4 7.7 %collective-permute-start.8 = (bf16[40,1024]{1,0:T(8,128)(2,1)S(1)}, bf16[40,1024]{1,0:T(8,128)(2,1)S(1)}, u32[]{:S(2)}, u32[]{:S(2)}) collective-permute-start(bf16[40,1024]{1,0:T(8,128)(2,1)S(1)} %get-tuple-element.15), channel_id=1, source_target_pairs={{0,8},{2,10},{4,12},{6,14},{8,0},{10,2},{12,4},{14,6},{1,9},{3,11}... | collective-permute-start | bytes 245768 | tf_op jit(solution)/shard_map/ppermute | solution.py:232
  34.4 7.8 %collective-permute-start.5 = (bf16[96,1024]{1,0:T(8,128)(2,1)}, bf16[96,1024]{1,0:T(8,128)(2,1)S(1)}, u32[]{:S(2)}, u32[]{:S(2)}) collective-permute-start(bf16[96,1024]{1,0:T(8,128)(2,1)} %get-tuple-element.10), channel_id=1, source_target_pairs={{0,1},{1,0},{2,3},{3,2},{4,5},{5,4},{6,7},{7,6},{8,9},{9,8},{10,11... | collective-permute-start | bytes 589832 | tf_op jit(solution)/shard_map/ppermute | solution.py:232
  42.1 4.5 %copy-start = (bf16[40,1024]{1,0:T(8,128)(2,1)}, bf16[40,1024]{1,0:T(8,128)(2,1)S(1)}, u32[]{:S(2)}) copy-start(bf16[40,1024]{1,0:T(8,128)(2,1)S(1)} %fusion.1.refs_2_) | copy-start | bytes 245764
  42.1 4.5 %collective-permute-start.10 = (bf16[40,1024]{1,0:T(8,128)(2,1)S(1)}, bf16[40,1024]{1,0:T(8,128)(2,1)S(1)}, u32[]{:S(2)}, u32[]{:S(2)}) collective-permute-start(bf16[40,1024]{1,0:T(8,128)(2,1)S(1)} %fusion.1.refs_2_), channel_id=1, source_target_pairs={{0,1},{1,0},{2,3},{3,2},{4,5},{5,4},{6,7},{7,6},{8,9},{9,8},{10,11... | collective-permute-start | bytes 245768 | tf_op jit(solution)/shard_map/ppermute | solution.py:232
  42.2 4.4 %copy-start.2 = (bf16[96,1024]{1,0:T(8,128)(2,1)}, bf16[96,1024]{1,0:T(8,128)(2,1)S(1)}, u32[]{:S(2)}) copy-start(bf16[96,1024]{1,0:T(8,128)(2,1)S(1)} %collective-permute-done.5) | copy-start | bytes 589828
  46.6 0.6 %copy-start.3 = (bf16[40,1024]{1,0:T(8,128)(2,1)}, bf16[40,1024]{1,0:T(8,128)(2,1)S(1)}, u32[]{:S(2)}) copy-start(bf16[40,1024]{1,0:T(8,128)(2,1)S(1)} %collective-permute-done.10.refs_3_) | copy-start | bytes 245764

commit v2 on v0

v2 whole, which is shorter than its diff:
```python
import functools

import jax
import jax.numpy as jnp
import ml_dtypes
import numpy as np
from jax import lax
from jax.experimental import pallas as pl
from jax.experimental.pallas import tpu as pltpu
from jax.sharding import PartitionSpec as P

NFFT = 4096
NF = 512
F0 = 8
PIECE = NFFT // 8
HALF = NFFT // 2
CHUNK = 256
F32 = jnp.float32
BF16 = jnp.bfloat16
LIMIT = 24 * 1024 * 1024


def piece_table():
    bins = F0 + np.arange(NF)
    angle = (bins * np.arange(PIECE)[:, None] % NFFT) * (2.0 * np.pi / NFFT)
    exact = np.concatenate([np.cos(angle), -np.sin(angle)], axis=1)
    high = exact.astype(ml_dtypes.bfloat16)
    low = (exact - high.astype(np.float64)).astype(ml_dtypes.bfloat16)
    return np.concatenate([high, low], axis=0)


def split_two(x):
    high = x.astype(BF16)
    low = (x - high.astype(F32)).astype(BF16)
    return high, low


def dot(a, b):
    return jnp.dot(a, b, preferred_element_type=F32)


def dot_three(x, table, rows):
    high, low = split_two(x)
    first = table[:rows, :]
    return dot(high, first) + dot(low, first) + dot(high, table[PIECE : PIECE + rows, :])


class Turns:
    def __init__(self):
        lane = lax.broadcasted_iota(jnp.int32, (1, CHUNK), 1)
        turn = lane % 4
        self.odd = (turn % 2) == 1
        self.sign = jnp.where(self.odd, -1.0, 1.0)
        self.real = jnp.where(turn < 2, 1.0, -1.0)
        self.imag = jnp.where((turn == 0) | (turn == 3), 1.0, -1.0)
        eighth = lane % 8
        root = np.float32(np.sqrt(0.5))
        self.cos = jnp.where(turn % 4 == 0, 1.0, jnp.where(turn == 2, 0.0, root))
        self.cos = jnp.where((eighth > 2) & (eighth < 6), -self.cos, self.cos)
        self.sin = jnp.where(turn == 2, 1.0, jnp.where(turn == 0, 0.0, root))
        self.sin = jnp.where(eighth < 4, -self.sin, self.sin)

    def quarter(self, ar, ai, br, bi):
        return (
            ar + self.real * jnp.where(self.odd, bi, br),
            ai + self.imag * jnp.where(self.odd, br, bi),
        )

    def half(self, re, im):
        ar, ai = self.quarter(re[0], im[0], re[2], im[2])
        br, bi = self.quarter(re[1], im[1], re[3], im[3])
        return ar + (br * self.cos - bi * self.sin), ai + (br * self.sin + bi * self.cos)


def half_spectra(x, table, channels, halves, turns, f):
    re = slice(f, f + CHUNK)
    im = slice(NF + f, NF + f + CHUNK)
    both = jnp.concatenate([x, x], axis=1)
    dr = dot(both, table[:, re])
    di = dot(both, table[:, im])
    out = []
    for b in range(halves):
        rows = [slice((4 * b + e) * channels, (4 * b + e + 1) * channels) for e in range(4)]
        out.append(turns.half([dr[r] for r in rows], [di[r] for r in rows]))
    return out


def turned_taps(taps, square):
    count, channels = taps.shape
    square[...] = jnp.zeros_like(square)
    square[:count, :channels] = taps[...]
    return square[...].T[:channels, :]


def end_terms(filter_taps, tap_count, before, after):
    lag = tap_count - 1
    channels = before[0].shape[0]
    apart = [b.astype(F32) - a.astype(F32) for b, a in zip(before, after)]
    width = apart[0].shape[1]
    lane = lax.broadcasted_iota(jnp.int32, (channels, width), 1)
    totals = [jnp.zeros((channels, width), F32) for _ in apart]
    for k in range(1, tap_count):
        tap = jnp.where(lane < k, filter_taps[:, k : k + 1], 0.0)
        for i, a in enumerate(apart):
            totals[i] = totals[i] + tap * pltpu.roll(a, k, 1)
    return [t[:, :lag] for t in totals]


def whiten_rows(re, im):
    rows = re.shape[0]
    place = lax.broadcasted_iota(jnp.int32, (rows, NF), 1)
    power = re * re + im * im
    smooth = power
    for s in (1, 2):
        smooth = smooth + jnp.where(place >= s, pltpu.roll(power, s, 1), 0.0)
        smooth = smooth + jnp.where(place < NF - s, pltpu.roll(power, NF - s, 1), 0.0)
    mean = jnp.mean(power, axis=1, keepdims=True)
    scaling = lax.rsqrt(smooth / 5.0 + 0.1 * mean + 1e-06)
    return (re * scaling).astype(BF16), (im * scaling).astype(BF16)


ROWS = 16


def whiten_all(spectra, white, count):
    def step(i, carry):
        rows = pl.ds(pl.multiple_of(i * ROWS, ROWS), ROWS)
        re, im = whiten_rows(spectra[rows, :NF], spectra[rows, NF:])
        white[rows, :NF] = re
        white[rows, NF:] = im
        return carry

    lax.fori_loop(0, count // ROWS, step, 0)


def own_kernel(windows, traces, taps, table, part, white, response, square, spectra):
    channels, samples = traces.shape
    tap_count = taps.shape[0]
    filter_taps = turned_taps(taps, square)
    response[...] = dot_three(filter_taps[:, :tap_count], table, tap_count)
    tile = 128
    last = windows - 1
    start = (last - 1) * HALF
    before = [traces[:, start - tile : start]]
    after = [traces[:, samples - tile :]]
    edge = end_terms(filter_taps, tap_count, before, after)[0]
    spectra[...] = dot_three(edge, table, tap_count - 1)
    pieces = samples // PIECE
    x = jnp.concatenate([traces[:, q * PIECE : (q + 1) * PIECE] for q in range(pieces)], axis=0)
    turns = Turns()
    for f in range(0, NF, CHUNK):
        re = slice(f, f + CHUNK)
        im = slice(NF + f, NF + f + CHUNK)
        halves = half_spectra(x, table, channels, windows, turns, f)
        pr, pi = response[:, re], response[:, im]
        for w in range(windows):
            xr, xi = halves[w]
            xr, xi = turns.sign * xr, turns.sign * xi
            if w > 0:
                xr, xi = xr + halves[w - 1][0], xi + halves[w - 1][1]
            yr = xr * pr - xi * pi
            yi = xr * pi + xi * pr
            if w < last:
                rows = slice(w * channels, (w + 1) * channels)
                part[rows, re] = yr
                part[rows, im] = yi
            else:
                spectra[:, re] = spectra[:, re] + yr
                spectra[:, im] = spectra[:, im] + yi
    whiten_all(spectra, white, channels)


def picks_kernel(shape, where, counts, slots, *refs):
    channels, windows, pairs, block_rows, chips, times = shape
    wanted, picks, chosen = refs[:chips], refs[chips], refs[chips + 1]
    group = where[0]
    first = jnp.int32(0)
    for g in range(counts.shape[0]):
        first = first + jnp.where(g < group, counts[g], 0)
    owned = counts[group]
    width = windows * channels
    column = lax.broadcasted_iota(jnp.int32, (1, width), 1) % channels
    base = 2 * chips * block_rows
    chosen[...] = jnp.zeros_like(chosen)
    for core in range(2):
        for d in range(chips):
            for p in range(pairs):
                slot = wanted[d][core, p] - first
                mine = (slot >= 0) & (slot < owned)
                channel = slots[group, jnp.where(mine, slot, 0)]
                line = (column == jnp.where(mine, channel, -1)).astype(F32)
                row = (core * chips + d) * block_rows + p
                for w in range(windows):
                    chosen[row + w * pairs : row + w * pairs + 1, :] = line
    block = lax.broadcasted_iota(jnp.int32, (block_rows, width), 0)
    window = lax.broadcasted_iota(jnp.int32, (block_rows, width), 1) // channels
    inside = (block >= window * pairs) & (block < (window + 1) * pairs)
    for b in range(2 * chips):
        rows = slice(b * block_rows, (b + 1) * block_rows)
        picks[rows, :] = jnp.where(inside, chosen[rows, :], 0.0).astype(BF16)
    part = channels // times
    count = windows * channels
    row = lax.broadcasted_iota(jnp.int32, (count, width), 0)
    col = lax.broadcasted_iota(jnp.int32, (count, width), 1)
    distance = row // (windows * part)
    line = (where[1] ^ distance) * part + row % part
    at = (row // part) % windows * channels + line
    picks[base : base + count, :] = (col == at).astype(F32).astype(BF16)


def rest_kernel(
    shape, traces, halo, taps, table, part, own_white, response, picks, *refs
):
    channels, windows, pairs, block_rows, chips, times = shape
    keep, send = refs[:2]
    blocks = refs[2 : 2 + times]
    square, spectra, white = refs[2 + times :]
    tap_count = taps.shape[0]
    filter_taps = turned_taps(taps, square)
    tile = halo.shape[1] - HALF
    before = [halo[:, :tile], halo[:, HALF:]]
    for b in range(1, windows - 2):
        before.append(traces[:, b * HALF - tile : b * HALF])
    after = [traces[:, (w + 1) * HALF - tile : (w + 1) * HALF] for w in range(windows - 1)]
    edges = end_terms(filter_taps, tap_count, before, after)
    spectra[...] = part[...] + dot_three(jnp.concatenate(edges, axis=0), table, tap_count - 1)
    x = jnp.concatenate(
        [halo[:, tile + q * PIECE : tile + (q + 1) * PIECE] for q in range(HALF // PIECE)],
        axis=0,
    )
    turns = Turns()
    for f in range(0, NF, CHUNK):
        re = slice(f, f + CHUNK)
        im = slice(NF + f, NF + f + CHUNK)
        xr, xi = half_spectra(x, table, channels, 1, turns, f)[0]
        pr, pi = response[:, re], response[:, im]
        spectra[:channels, re] = spectra[:channels, re] + (xr * pr - xi * pi)
        spectra[:channels, im] = spectra[:channels, im] + (xr * pi + xi * pr)
    count = (windows - 1) * channels
    whiten_all(spectra, white, count)
    white[count:, :] = own_white[...]
    base = 2 * chips * block_rows
    rows = windows * channels // times
    choose = picks[...]
    for f in range(0, 2 * NF, CHUNK):
        cols = slice(f, f + CHUNK)
        out = dot(choose, white[:, cols]).astype(BF16)
        keep[:, cols] = out[: base // 2]
        send[:, cols] = out[base // 2 : base]
        for d in range(times):
            blocks[d][:, cols] = out[base + d * rows : base + (d + 1) * rows]


def correlate_kernel(windows, factor, count, has_total, *refs):
    receivers = refs[:count]
    sources = refs[count : 2 * count]
    total = refs[2 * count] if has_total else None
    out, line_r, line_s = refs[2 * count + has_total :]
    step, part = out.shape[0], out.shape[1]
    pairs = line_s.shape[0]

    @pl.when(pl.program_id(0) == 0)
    def _():
        for d in range(count):
            for w in range(windows):
                at = d * windows + w
                line_r[at] = receivers[d][w].astype(F32) * factor
                rows = sources[d][w * pairs : (w + 1) * pairs, :].astype(F32)
                for p in range(pairs):
                    line_s[p, at : at + 1, :] = rows[p : p + 1, :]

    start = pl.program_id(0) * step
    for i in range(step):
        for f in range(0, NF, 128):
            re = slice(f, f + 128)
            im = slice(NF + f, NF + f + 128)
            if has_total:
                total_r, total_i = total[i, :, re], total[i, :, im]
            else:
                total_r = jnp.zeros((part, 128), F32)
                total_i = jnp.zeros((part, 128), F32)
            for at in range(count * windows):
                rr = line_r[at, :, re]
                ri = line_r[at, :, im]
                sr = line_s[start + i, at : at + 1, re]
                si = line_s[start + i, at : at + 1, im]
                total_r = total_r + (sr * rr + si * ri)
                total_i = total_i + (sr * ri - si * rr)
            out[i, :, re] = total_r
            out[i, :, im] = total_i


def correlate(receivers, sources, total, pairs, factor):
    windows, part, width = receivers[0].shape
    count = len(receivers)
    step = next(s for s in (2, 1) if pairs % s == 0)
    block = pl.BlockSpec((step, part, width), lambda i: (i, 0, 0))
    extra = [] if total is None else [total]
    return pl.pallas_call(
        functools.partial(correlate_kernel, windows, factor, count, len(extra)),
        out_shape=jax.ShapeDtypeStruct((pairs, part, width), F32),
        grid=(pairs // step,),
        in_specs=[pl.BlockSpec(r.shape, lambda i: (0, 0, 0)) for r in receivers]
        + [pl.BlockSpec(s.shape, lambda i: (0, 0)) for s in sources]
        + [block] * len(extra),
        out_specs=block,
        scratch_shapes=[
            pltpu.VMEM((count * windows, part, width), F32),
            pltpu.VMEM((pairs, -(-count * windows // 8) * 8, width), F32),
        ],
        compiler_params=pltpu.CompilerParams(vmem_limit_bytes=LIMIT),
        name="correlate",
    )(*receivers, *sources, *extra)


def shards(traces, filter_taps, source_counts, source_channel, block_sources):
    channels, samples = traces.shape
    tap_count = filter_taps.shape[1]
    pairs = block_sources.shape[1]
    windows = samples // HALF
    groups = lax.axis_size("chan")
    times = lax.axis_size("tm")
    chips = groups // 2
    part = channels // times
    block_rows = -(-windows * pairs // 8) * 8

    def across(x, axis, distance):
        size = lax.axis_size(axis)
        return lax.ppermute(x, axis, [(i, i ^ distance) for i in range(size)])

    tail = traces[:, samples - HALF - 128 :]
    halo = lax.ppermute(tail, "tm", [(i - 1, i) for i in range(1, times)])
    both = jnp.concatenate([block_sources, across(block_sources, "chan", 1)], axis=0)
    wanted = [both] + [across(both, "chan", 2 * d) for d in range(1, chips)]
    where = jnp.stack([lax.axis_index("chan"), lax.axis_index("tm")]).astype(jnp.int32)

    shape = (channels, windows, pairs, block_rows, chips, times)
    smem = pl.BlockSpec(memory_space=pltpu.SMEM)
    vmem = pl.BlockSpec(memory_space=pltpu.VMEM)
    params = pltpu.CompilerParams(vmem_limit_bytes=LIMIT)
    width = windows * channels
    all_rows = 2 * chips * block_rows + width
    taps = filter_taps.T
    table = jnp.asarray(piece_table())
    part_spectra, own_white, response = pl.pallas_call(
        functools.partial(own_kernel, windows),
        out_shape=[
            jax.ShapeDtypeStruct((width - channels, 2 * NF), F32),
            jax.ShapeDtypeStruct((channels, 2 * NF), BF16),
            jax.ShapeDtypeStruct((channels, 2 * NF), F32),
        ],
        in_specs=[vmem] * 3,
        out_specs=[vmem] * 3,
        scratch_shapes=[pltpu.VMEM((128, 128), F32), pltpu.VMEM((channels, 2 * NF), F32)],
        compiler_params=params,
        name="own",
    )(traces, taps, table)
    picks = pl.pallas_call(
        functools.partial(picks_kernel, shape),
        out_shape=jax.ShapeDtypeStruct((all_rows, width), BF16),
        in_specs=[smem] * (3 + chips),
        out_specs=vmem,
        scratch_shapes=[pltpu.VMEM((2 * chips * block_rows, width), F32)],
        compiler_params=params,
        name="picks",
    )(where, source_counts, source_channel, *wanted)
    outs = pl.pallas_call(
        functools.partial(rest_kernel, shape),
        out_shape=[jax.ShapeDtypeStruct((chips * block_rows, 2 * NF), BF16)] * 2
        + [jax.ShapeDtypeStruct((windows * part, 2 * NF), BF16)] * times,
        in_specs=[vmem] * 8,
        out_specs=[vmem] * (2 + times),
        scratch_shapes=[
            pltpu.VMEM((128, 128), F32),
            pltpu.VMEM((width - channels, 2 * NF), F32),
            pltpu.VMEM((width, 2 * NF), BF16),
        ],
        compiler_params=params,
        name="rest",
    )(traces, halo, taps, table, part_spectra, own_white, response, picks)
    keep, send, blocks = outs[0], outs[1], outs[2:]
    gathered = keep + across(send, "chan", 1)
    pieces = [gathered[d * block_rows : (d + 1) * block_rows] for d in range(chips)]
    mine = pieces[0]
    for d in range(1, chips):
        mine = mine + across(pieces[d], "chan", 2 * d)
    receivers = [blocks[0]] + [across(blocks[d], "tm", d) for d in range(1, times)]
    receivers = [r.reshape(windows, part, 2 * NF) for r in receivers]
    sources = [mine] + [across(mine, "tm", d) for d in range(1, times)]

    factor = 1.0 / (windows * times)
    total = correlate(receivers[:1], sources[:1], None, pairs, factor)
    if times > 1:
        total = correlate(receivers[1:], sources[1:], total, pairs, factor)
    return total.transpose(1, 0, 2)


def solution(mesh):
    in_specs = (P(("seg", "chan"), "tm"), P("chan", None), P(), P(), P("chan", None))
    out_specs = P(("seg", "chan", "tm"), None, None)
    return jax.shard_map(shards, mesh=mesh, in_specs=in_specs, out_specs=out_specs, check_vma=False)
```

time: 171 us -> 46.7 us (0.27)
  other arithmetic: 60.5 us -> 0.2 us
  waiting for transfers between devices: 72.8 us -> 16.5 us
  between operations: 13.6 us -> 0.17 us
  Pallas kernels: 0 us -> 11.8 us
  local copies, waits for them, and re-layouts: 13.1 us -> 4.46 us
  starting transfers between devices: 4.93 us -> 13.2 us
  matrix products: 5.69 us -> 0 us
    convert_element_type x4 -> x0, other arithmetic: 53.6 us -> none  [the longest x1 35 us: transform_table(): cosine = jnp.cos(angles).astype(jnp.bfloat16)]
    reduce_scatter x1 -> x0, waiting for transfers between devices: 42.8 us -> none  [shards(): lax.psum_scatter(correlate(receivers[:, None], sources, factor), 'tm', sc...]
    all_gather x1 -> x0, waiting for transfers between devices: 29.9 us -> none  [shards(): everything = lax.all_gather(slot_rows, 'chan', axis=0, tiled=True)]
    ppermute x1 -> x11, waiting for transfers between devices: 0.01 us -> 16.5 us  [the longest x10 16.5 us: across(): return lax.ppermute(x, axis, [(i, i ^ distance) for i in range(size)])]
    pallas_call x0 -> x5, Pallas kernels: none -> 11.8 us  [the longest x1 3.67 us: shards(): pl.pallas_call(functools.partial(rest_kernel, shape), out_shape=[jax.Shap...]
    ppermute x1 -> x11, starting transfers between devices: 4.89 us -> 13.2 us  [the longest x10 8.22 us: across(): return lax.ppermute(x, axis, [(i, i ^ distance) for i in range(size)])]
    dot_general x1 -> x0, matrix products: 5.69 us -> none  [shards(): jnp.dot(windows, transform_table(), preferred_element_type=jnp.float32)]
    gather x3 -> x0, local copies, waits for them, and re-layouts: 4.52 us -> none  [the longest x1 2.29 us: shards(): picked = everything[home_group * slot_count + slot_index]]
  transfers between devices with their start and end apart: 3 -> 11, of which waited for: 2 -> 7; matrix products, arithmetic and copies ran while one was open for 23% -> 0% of each run, Pallas kernels for 0% -> 12%
where the time goes in v2:
time: 46.7 us; the launch traced here: 46.4 us
  waiting for transfers between devices  16.5 us (35%)
  starting transfers between devices  13.2 us (28%)
  Pallas kernels  11.8 us (25%)
  local copies, waits for them, and re-layouts  4.46 us (10%)
    ppermute x10, waiting for transfers between devices, across(): return lax.ppermute(x, axis, [(i, i ^ distance) for i in range(size)])  16.5 us
    ppermute x10, starting transfers between devices, across(): return lax.ppermute(x, axis, [(i, i ^ distance) for i in range(size)])  8.22 us
    ppermute x1, starting transfers between devices, shards(): halo = lax.ppermute(tail, 'tm', [(i - 1, i) for i in range(1, times)])  5.02 us
    pallas_call x1, Pallas kernels, shards(): pl.pallas_call(functools.partial(rest_kernel, shape), out_shape=[jax.Shap...  3.67 us
    pallas_call x2, Pallas kernels, correlate(): pl.pallas_call(functools.partial(correlate_kernel, windows, factor, count...  3.52 us
    pallas_call x1, Pallas kernels, shards(): pl.pallas_call(functools.partial(own_kernel, windows), out_shape=[jax.Sha...  3.48 us
    unnamed x14, local copies, waits for them, and re-layouts  3.47 us
    pallas_call x1, Pallas kernels, shards(): pl.pallas_call(functools.partial(picks_kernel, shape), out_shape=jax.Shap...  1.14 us
  transfers between devices with their start and end apart: 11, of which 7 were waited for; matrix products, arithmetic and copies ran while one was open for 0% of the time, Pallas kernels for 12%

profile of v2, /device:TPU:0, one launch (start us, length us, event | category | flops | bytes accessed | tf_op | source)
XLA Modules:
  0.0 46.4 jit_solution(10797660355072896007)
XLA Ops:
  0.0 1.0 %slice.15 = bf16[64,2176]{1,0:T(8,128)(2,1)S(1)} slice(bf16[64,6144]{1,0:T(8,128)(2,1)} %traces.3), slice={[0:64], [3968:6144]} | slice | bytes 557056 | tf_op jit(solution)/shard_map/slice | solution.py:331
  1.0 0.0 copy-start.6
  1.0 0.0 copy-start.4
  1.0 0.0 copy-start.5
  1.0 5.0 %collective-permute-start = (bf16[64,2176]{1,0:T(8,128)(2,1)S(1)}, bf16[64,2176]{1,0:T(8,128)(2,1)S(1)}, u32[]{:S(2)}, u32[]{:S(2)}) collective-permute-start(bf16[64,2176]{1,0:T(8,128)(2,1)S(1)} %slice.15), channel_id=1, source_target_pairs={{0,1},{2,3},{4,5},{6,7},{8,9},{10,11},{12,13},{14,15},{16,17},{18,... | collective-permute-start | bytes 835592 | tf_op jit(solution)/shard_map/ppermute | solution.py:332
  6.0 0.1 collective-permute-start.1
  6.1 0.0 copy-start
  6.1 1.6 %copy-done = bf16[1024,1024]{1,0:T(8,128)(2,1)S(1)} copy-done((bf16[1024,1024]{1,0:T(8,128)(2,1)S(1)}, bf16[1024,1024]{1,0:T(8,128)(2,1)}, u32[]{:S(2)}) %copy-start) | copy-done | bytes 2097176
  7.7 0.0 copy-start.1
  7.7 1.1 %copy-done.1 = bf16[64,6144]{1,0:T(8,128)(2,1)S(1)} copy-done((bf16[64,6144]{1,0:T(8,128)(2,1)S(1)}, bf16[64,6144]{1,0:T(8,128)(2,1)}, u32[]{:S(2)}) %copy-start.1) | copy-done | bytes 786456
  8.9 0.0 copy-start.3
  8.9 0.7 %copy-done.3 = f32[64,33]{0,1:T(8,128)S(1)} copy-done((f32[64,33]{0,1:T(8,128)S(1)}, f32[64,33]{0,1:T(8,128)}, u32[]{:S(2)}) %copy-start.3) | copy-done | bytes 8472
  9.6 0.0 copy-start.2
  9.6 3.5 %own.1 = (f32[128,1024]{1,0:T(8,128)S(1)}, bf16[64,1024]{1,0:T(8,128)(2,1)S(1)}, f32[64,1024]{1,0:T(8,128)S(1)}) custom-call(bf16[64,6144]{1,0:T(8,128)(2,1)S(1)} %copy-done.1, f32[33,64]{1,0:T(8,128)S(1)} %bitcast.8, bf16[1024,1024]{1,0:T(8,128)(2,1)S(1)} %copy-done), custom_call_target="tpu_custom_call" | custom-call | tf_op jit(solution)/shard_map/own/pallas_call | solution.py:345
  13.1 0.1 pad_add_fusion.1.where
  13.2 0.0 collective-permute-done.1
  13.2 0.0 copy-done.6
  13.2 3.7 %collective-permute-start.4 = (s32[2,12]{1,0:T(2,128)S(1)}, s32[2,12]{1,0:T(2,128)S(1)}, u32[]{:S(2)}, u32[]{:S(2)}) collective-permute-start(s32[2,12]{1,0:T(2,128)S(1)} %pad_add_fusion.refs_0_), channel_id=1, source_target_pairs={{0,12},{2,14},{4,8},{6,10},{8,4},{10,6},{12,0},{14,2},{1,13},{3,15... | collective-permute-start | bytes 296 | tf_op jit(solution)/shard_map/ppermute | solution.py:329
  16.8 0.0 collective-permute-start.3
  16.8 0.8 %collective-permute-start.2 = (s32[2,12]{1,0:T(2,128)S(1)}, s32[2,12]{1,0:T(2,128)S(1)}, u32[]{:S(2)}, u32[]{:S(2)}) collective-permute-start(s32[2,12]{1,0:T(2,128)S(1)} %pad_add_fusion.refs_0_), channel_id=1, source_target_pairs={{0,4},{2,6},{4,0},{6,2},{8,12},{10,14},{12,8},{14,10},{1,5},{3,7},... | collective-permute-start | bytes 296 | tf_op jit(solution)/shard_map/ppermute | solution.py:329
  17.6 1.0 %collective-permute-done.4.refs_3_ = s32[2,12]{1,0:T(2,128)S(1)} collective-permute-done((s32[2,12]{1,0:T(2,128)S(1)}, s32[2,12]{1,0:T(2,128)S(1)}, u32[]{:S(2)}, u32[]{:S(2)}) %collective-permute-start.4) | collective-permute-done | bytes 128 | tf_op jit(solution)/shard_map/ppermute | solution.py:329
  18.6 2.7 %collective-permute-done.3.refs_2_ = s32[2,12]{1,0:T(2,128)S(1)} collective-permute-done((s32[2,12]{1,0:T(2,128)S(1)}, s32[2,12]{1,0:T(2,128)S(1)}, u32[]{:S(2)}, u32[]{:S(2)}) %collective-permute-start.3) | collective-permute-done | bytes 128 | tf_op jit(solution)/shard_map/ppermute | solution.py:329
  21.3 0.0 collective-permute-done.2.refs_1_
  21.3 0.0 copy-done.4
  21.3 0.0 copy-done.5
  21.3 1.1 %picks.1 = bf16[512,192]{1,0:T(8,128)(2,1)S(1)} custom-call(s32[2]{0:T(128)S(1)} %pad_add_fusion.1.where, s32[8]{0:T(128)S(1)} %copy-done.5, s32[8,36]{1,0:T(8,128)S(1)} %copy-done.4, s32[2,12]{1,0:T(2,128)S(1)} %pad_add_fusion.refs_0_, s32[2,12]{1,0:T(2,128)S(1)} %collective-permute-done.2.refs_1_, s32[2,12]{1,0:T(2,128)S(1)} %collective-permute-done.3.refs_2_, ...), custom_call_target="tpu_custom_call" | custom-call | tf_op jit(solution)/shard_map/picks/pallas_call | solution.py:358
  22.5 0.0 collective-permute-done.halo
  22.5 0.0 copy-done.2
  22.5 3.7 %rest.1 = (bf16[160,1024]{1,0:T(8,128)(2,1)S(1)}, bf16[160,1024]{1,0:T(8,128)(2,1)S(1)}, bf16[96,1024]{1,0:T(8,128)(2,1)S(1)}, bf16[96,1024]{1,0:T(8,128)(2,1)S(1)}) custom-call(bf16[64,6144]{1,0:T(8,128)(2,1)S(1)} %copy-done.2, bf16[64,2176]{1,0:T(8,128)(2,1)S(1)} %collective-permute-done.halo, f32[33,64]{1,0:T(8,128)S(1)} %bitcast.9, ...), custom_call_target="tpu_custom_call" | custom-call | tf_op jit(solution)/shard_map/rest/pallas_call | solution.py:367
  26.2 0.1 collective-permute-start.6
  26.2 1.6 %collective-permute-done.6 = bf16[160,1024]{1,0:T(8,128)(2,1)S(1)} collective-permute-done((bf16[160,1024]{1,0:T(8,128)(2,1)S(1)}, bf16[160,1024]{1,0:T(8,128)(2,1)S(1)}, u32[]{:S(2)}, u32[]{:S(2)}) %collective-permute-start.6) | collective-permute-done | bytes 327712 | tf_op jit(solution)/shard_map/ppermute | solution.py:329
  27.9 0.1 add.12
  28.0 0.1 collective-permute-start.7
  28.1 3.5 %collective-permute-start.9 = (bf16[40,1024]{1,0:T(8,128)(2,1)S(1)}, bf16[40,1024]{1,0:T(8,128)(2,1)S(1)}, u32[]{:S(2)}, u32[]{:S(2)}) collective-permute-start(bf16[40,1024]{1,0:T(8,128)(2,1)S(1)} %get-tuple-element.20), channel_id=1, source_target_pairs={{0,12},{2,14},{4,8},{6,10},{8,4},{10,6},{12,0},{14,2},{1,13},{3,15... | collective-permute-start | bytes 245768 | tf_op jit(solution)/shard_map/ppermute | solution.py:329
  31.5 0.0 collective-permute-start.8
  31.5 0.0 collective-permute-start.5
  31.5 1.0 %collective-permute-done.7 = bf16[40,1024]{1,0:T(8,128)(2,1)S(1)} collective-permute-done((bf16[40,1024]{1,0:T(8,128)(2,1)S(1)}, bf16[40,1024]{1,0:T(8,128)(2,1)S(1)}, u32[]{:S(2)}, u32[]{:S(2)}) %collective-permute-start.7) | collective-permute-done | bytes 81952 | tf_op jit(solution)/shard_map/ppermute | solution.py:329
  32.5 4.1 %collective-permute-done.9 = bf16[40,1024]{1,0:T(8,128)(2,1)S(1)} collective-permute-done((bf16[40,1024]{1,0:T(8,128)(2,1)S(1)}, bf16[40,1024]{1,0:T(8,128)(2,1)S(1)}, u32[]{:S(2)}, u32[]{:S(2)}) %collective-permute-start.9) | collective-permute-done | bytes 81952 | tf_op jit(solution)/shard_map/ppermute | solution.py:329
  36.7 2.5 %collective-permute-done.8 = bf16[40,1024]{1,0:T(8,128)(2,1)S(1)} collective-permute-done((bf16[40,1024]{1,0:T(8,128)(2,1)S(1)}, bf16[40,1024]{1,0:T(8,128)(2,1)S(1)}, u32[]{:S(2)}, u32[]{:S(2)}) %collective-permute-start.8) | collective-permute-done | bytes 81952 | tf_op jit(solution)/shard_map/ppermute | solution.py:329
  39.2 0.1 collective-permute-start.10
  39.3 0.9 %correlate.2.refs_2_ = f32[12,32,1024]{2,1,0:T(8,128)S(1)} custom-call(bf16[3,32,1024]{2,1,0:T(8,128)(2,1)S(1)} %bitcast.6, bf16[40,1024]{1,0:T(8,128)(2,1)S(1)} %fusion.1.refs_1_), custom_call_target="tpu_custom_call" | custom-call | tf_op jit(solution)/shard_map/correlate/pallas_call | solution.py:299
  40.2 0.0 collective-permute-done.5
  40.2 3.5 %collective-permute-done.10.refs_1_ = bf16[40,1024]{1,0:T(8,128)(2,1)S(1)} collective-permute-done((bf16[40,1024]{1,0:T(8,128)(2,1)S(1)}, bf16[40,1024]{1,0:T(8,128)(2,1)S(1)}, u32[]{:S(2)}, u32[]{:S(2)}) %collective-permute-start.10) | collective-permute-done | bytes 81952 | tf_op jit(solution)/shard_map/ppermute | solution.py:329
  43.8 2.6 %correlate.3 = f32[12,32,1024]{2,1,0:T(8,128)} custom-call(bf16[3,32,1024]{2,1,0:T(8,128)(2,1)S(1)} %bitcast.7, bf16[40,1024]{1,0:T(8,128)(2,1)S(1)} %collective-permute-done.10.refs_1_, f32[12,32,1024]{2,1,0:T(8,128)S(1)} %correlate.2.refs_2_), custom_call_target="tpu_custom_call" | custom-call | tf_op jit(solution)/shard_map/correlate/pallas_call | solution.py:299
  (3 shorter events, 0.0 us)
Async XLA Ops:
  1.0 12.2 %copy-start.6 = (s32[1,12]{1,0:T(1,128)S(1)}, s32[1,12]{1,0:T(1,128)}, u32[]{:S(2)}) copy-start(s32[1,12]{1,0:T(1,128)} %param.10) | copy-start | bytes 148
  1.0 20.3 %copy-start.4 = (s32[8,36]{1,0:T(8,128)S(1)}, s32[8,36]{1,0:T(8,128)}, u32[]{:S(2)}) copy-start(s32[8,36]{1,0:T(8,128)} %slots.1) | copy-start | bytes 3460
  1.0 20.3 %copy-start.5 = (s32[8]{0:T(128)S(1)}, s32[8]{0:T(128)}, u32[]{:S(2)}) copy-start(s32[8]{0:T(128)} %counts.1) | copy-start | bytes 100
  1.0 21.5 %collective-permute-start = (bf16[64,2176]{1,0:T(8,128)(2,1)S(1)}, bf16[64,2176]{1,0:T(8,128)(2,1)S(1)}, u32[]{:S(2)}, u32[]{:S(2)}) collective-permute-start(bf16[64,2176]{1,0:T(8,128)(2,1)S(1)} %slice.15), channel_id=1, source_target_pairs={{0,1},{2,3},{4,5},{6,7},{8,9},{10,11},{12,13},{14,15},{16,17},{18,... | collective-permute-start | bytes 835592 | tf_op jit(solution)/shard_map/ppermute | solution.py:332
  6.0 7.1 %collective-permute-start.1 = (s32[1,12]{1,0:T(1,128)}, s32[1,12]{1,0:T(1,128)S(1)}, u32[]{:S(2)}, u32[]{:S(2)}) collective-permute-start(s32[1,12]{1,0:T(1,128)} %param.10), channel_id=1, source_target_pairs={{0,2},{2,0},{4,6},{6,4},{8,10},{10,8},{12,14},{14,12},{1,3},{3,1},... | collective-permute-start | bytes 152 | tf_op jit(solution)/shard_map/ppermute | solution.py:329
  6.1 1.6 %copy-start = (bf16[1024,1024]{1,0:T(8,128)(2,1)S(1)}, bf16[1024,1024]{1,0:T(8,128)(2,1)}, u32[]{:S(2)}) copy-start(bf16[1024,1024]{1,0:T(8,128)(2,1)} %constant.10.clone.table) | copy-start | bytes 6291460
  7.7 1.1 %copy-start.1 = (bf16[64,6144]{1,0:T(8,128)(2,1)S(1)}, bf16[64,6144]{1,0:T(8,128)(2,1)}, u32[]{:S(2)}) copy-start(bf16[64,6144]{1,0:T(8,128)(2,1)} %traces.3) | copy-start | bytes 2359300
  8.9 0.7 %copy-start.3 = (f32[64,33]{0,1:T(8,128)S(1)}, f32[64,33]{0,1:T(8,128)}, u32[]{:S(2)}) copy-start(f32[64,33]{0,1:T(8,128)} %param.7) | copy-start | bytes 25348
  9.6 12.9 %copy-start.2 = (bf16[64,6144]{1,0:T(8,128)(2,1)S(1)}, bf16[64,6144]{1,0:T(8,128)(2,1)}, u32[]{:S(2)}) copy-start(bf16[64,6144]{1,0:T(8,128)(2,1)} %traces.3) | copy-start | bytes 2359300
  13.2 5.4 %collective-permute-start.4 = (s32[2,12]{1,0:T(2,128)S(1)}, s32[2,12]{1,0:T(2,128)S(1)}, u32[]{:S(2)}, u32[]{:S(2)}) collective-permute-start(s32[2,12]{1,0:T(2,128)S(1)} %pad_add_fusion.refs_0_), channel_id=1, source_target_pairs={{0,12},{2,14},{4,8},{6,10},{8,4},{10,6},{12,0},{14,2},{1,13},{3,15... | collective-permute-start | bytes 296 | tf_op jit(solution)/shard_map/ppermute | solution.py:329
  16.8 4.5 %collective-permute-start.3 = (s32[2,12]{1,0:T(2,128)S(1)}, s32[2,12]{1,0:T(2,128)S(1)}, u32[]{:S(2)}, u32[]{:S(2)}) collective-permute-start(s32[2,12]{1,0:T(2,128)S(1)} %pad_add_fusion.refs_0_), channel_id=1, source_target_pairs={{0,8},{2,10},{4,12},{6,14},{8,0},{10,2},{12,4},{14,6},{1,9},{3,11}... | collective-permute-start | bytes 296 | tf_op jit(solution)/shard_map/ppermute | solution.py:329
  16.8 4.5 %collective-permute-start.2 = (s32[2,12]{1,0:T(2,128)S(1)}, s32[2,12]{1,0:T(2,128)S(1)}, u32[]{:S(2)}, u32[]{:S(2)}) collective-permute-start(s32[2,12]{1,0:T(2,128)S(1)} %pad_add_fusion.refs_0_), channel_id=1, source_target_pairs={{0,4},{2,6},{4,0},{6,2},{8,12},{10,14},{12,8},{14,10},{1,5},{3,7},... | collective-permute-start | bytes 296 | tf_op jit(solution)/shard_map/ppermute | solution.py:329
  26.2 1.7 %collective-permute-start.6 = (bf16[160,1024]{1,0:T(8,128)(2,1)S(1)}, bf16[160,1024]{1,0:T(8,128)(2,1)S(1)}, u32[]{:S(2)}, u32[]{:S(2)}) collective-permute-start(bf16[160,1024]{1,0:T(8,128)(2,1)S(1)} %get-tuple-element.17), channel_id=1, source_target_pairs={{0,2},{2,0},{4,6},{6,4},{8,10},{10,8},{12,14},{14,12},{1,3},{3,1},... | collective-permute-start | bytes 983048 | tf_op jit(solution)/shard_map/ppermute | solution.py:329
  28.0 4.6 %collective-permute-start.7 = (bf16[40,1024]{1,0:T(8,128)(2,1)S(1)}, bf16[40,1024]{1,0:T(8,128)(2,1)S(1)}, u32[]{:S(2)}, u32[]{:S(2)}) collective-permute-start(bf16[40,1024]{1,0:T(8,128)(2,1)S(1)} %get-tuple-element.19), channel_id=1, source_target_pairs={{0,4},{2,6},{4,0},{6,2},{8,12},{10,14},{12,8},{14,10},{1,5},{3,7},... | collective-permute-start | bytes 245768 | tf_op jit(solution)/shard_map/ppermute | solution.py:329
  28.1 8.6 %collective-permute-start.9 = (bf16[40,1024]{1,0:T(8,128)(2,1)S(1)}, bf16[40,1024]{1,0:T(8,128)(2,1)S(1)}, u32[]{:S(2)}, u32[]{:S(2)}) collective-permute-start(bf16[40,1024]{1,0:T(8,128)(2,1)S(1)} %get-tuple-element.20), channel_id=1, source_target_pairs={{0,12},{2,14},{4,8},{6,10},{8,4},{10,6},{12,0},{14,2},{1,13},{3,15... | collective-permute-start | bytes 245768 | tf_op jit(solution)/shard_map/ppermute | solution.py:329
  31.5 7.7 %collective-permute-start.8 = (bf16[40,1024]{1,0:T(8,128)(2,1)S(1)}, bf16[40,1024]{1,0:T(8,128)(2,1)S(1)}, u32[]{:S(2)}, u32[]{:S(2)}) collective-permute-start(bf16[40,1024]{1,0:T(8,128)(2,1)S(1)} %get-tuple-element.21), channel_id=1, source_target_pairs={{0,8},{2,10},{4,12},{6,14},{8,0},{10,2},{12,4},{14,6},{1,9},{3,11}... | collective-permute-start | bytes 245768 | tf_op jit(solution)/shard_map/ppermute | solution.py:329
  31.5 8.7 %collective-permute-start.5 = (bf16[96,1024]{1,0:T(8,128)(2,1)S(1)}, bf16[96,1024]{1,0:T(8,128)(2,1)S(1)}, u32[]{:S(2)}, u32[]{:S(2)}) collective-permute-start(bf16[96,1024]{1,0:T(8,128)(2,1)S(1)} %get-tuple-element.15), channel_id=1, source_target_pairs={{0,1},{1,0},{2,3},{3,2},{4,5},{5,4},{6,7},{7,6},{8,9},{9,8},{10,11... | collective-permute-start | bytes 589832 | tf_op jit(solution)/shard_map/ppermute | solution.py:329
  39.2 4.5 %collective-permute-start.10 = (bf16[40,1024]{1,0:T(8,128)(2,1)S(1)}, bf16[40,1024]{1,0:T(8,128)(2,1)S(1)}, u32[]{:S(2)}, u32[]{:S(2)}) collective-permute-start(bf16[40,1024]{1,0:T(8,128)(2,1)S(1)} %fusion.1.refs_1_), channel_id=1, source_target_pairs={{0,1},{1,0},{2,3},{3,2},{4,5},{5,4},{6,7},{7,6},{8,9},{9,8},{10,11... | collective-permute-start | bytes 245768 | tf_op jit(solution)/shard_map/ppermute | solution.py:329

commit v3 on v2

--- a/solution.py
+++ b/solution.py
@@ -8,6 +8,7 @@
 from jax.experimental import pallas as pl
 from jax.experimental.pallas import tpu as pltpu
 from jax.sharding import PartitionSpec as P
+
 
 NFFT = 4096
 NF = 512
@@ -39,10 +40,10 @@
     return jnp.dot(a, b, preferred_element_type=F32)
 
 
-def dot_three(x, table, rows):
-    high, low = split_two(x)
-    first = table[:rows, :]
-    return dot(high, first) + dot(low, first) + dot(high, table[PIECE : PIECE + rows, :])
+def dot_three(x, table, rows, cols):
+    high, low = x
+    first = table[:rows, cols]
+    return dot(high, first) + dot(low, first) + dot(high, table[PIECE : PIECE + rows, cols])
 
 
 class Turns:
@@ -85,25 +86,16 @@
     return out
 
 
-def turned_taps(taps, square):
-    count, channels = taps.shape
-    square[...] = jnp.zeros_like(square)
-    square[:count, :channels] = taps[...]
-    return square[...].T[:channels, :]
-
-
-def end_terms(filter_taps, tap_count, before, after):
+def end_terms(taps_wide, shifted, tap_count, ends):
     lag = tap_count - 1
-    channels = before[0].shape[0]
-    apart = [b.astype(F32) - a.astype(F32) for b, a in zip(before, after)]
-    width = apart[0].shape[1]
-    lane = lax.broadcasted_iota(jnp.int32, (channels, width), 1)
-    totals = [jnp.zeros((channels, width), F32) for _ in apart]
-    for k in range(1, tap_count):
-        tap = jnp.where(lane < k, filter_taps[:, k : k + 1], 0.0)
-        for i, a in enumerate(apart):
-            totals[i] = totals[i] + tap * pltpu.roll(a, k, 1)
-    return [t[:, :lag] for t in totals]
+    apart = ends.T
+    size = apart.shape[0]
+    shifted[...] = jnp.zeros_like(shifted)
+    shifted[:tap_count, :] = taps_wide
+    total = jnp.zeros((lag, apart.shape[1]), F32)
+    for j in range(1, tap_count):
+        total = total + shifted[j : j + lag, :] * apart[size - j : size - j + 1, :]
+    return total.T
 
 
 def whiten_rows(re, im):
@@ -114,8 +106,8 @@
     for s in (1, 2):
         smooth = smooth + jnp.where(place >= s, pltpu.roll(power, s, 1), 0.0)
         smooth = smooth + jnp.where(place < NF - s, pltpu.roll(power, NF - s, 1), 0.0)
-    mean = jnp.mean(power, axis=1, keepdims=True)
-    scaling = lax.rsqrt(smooth / 5.0 + 0.1 * mean + 1e-06)
+    total = jnp.sum(power, axis=1, keepdims=True)
+    scaling = lax.rsqrt(smooth * 0.2 + (total * (0.1 / NF) + 1e-06))
     return (re * scaling).astype(BF16), (im * scaling).astype(BF16)
 
 
@@ -130,29 +122,65 @@
         white[rows, NF:] = im
         return carry
 
-    lax.fori_loop(0, count // ROWS, step, 0)
-
-
-def own_kernel(windows, traces, taps, table, part, white, response, square, spectra):
+    lax.fori_loop(0, count // ROWS, step, 0, unroll=2)
+
+
+def own_kernel(
+    windows,
+    traces_in,
+    taps_in,
+    table_in,
+    part,
+    white,
+    response,
+    ends,
+    taps,
+    table,
+    traces,
+    square,
+    shifted,
+    spectra,
+    sems,
+):
     channels, samples = traces.shape
     tap_count = taps.shape[0]
-    filter_taps = turned_taps(taps, square)
-    response[...] = dot_three(filter_taps[:, :tap_count], table, tap_count)
+    copies = [
+        pltpu.make_async_copy(taps_in, taps, sems.at[0]),
+        pltpu.make_async_copy(traces_in, traces, sems.at[1]),
+    ]
+    order = [c for f in range(0, NF, CHUNK) for c in (f, NF + f)]
+    for i, c in enumerate(order):
+        cols = slice(c, c + CHUNK)
+        copies.append(
+            pltpu.make_async_copy(table_in.at[:, cols], table.at[:, cols], sems.at[2 + i])
+        )
+    for copy in copies:
+        copy.start()
+    copies[0].wait()
+    square[...] = jnp.zeros_like(square)
+    square[:tap_count, :channels] = taps[...]
+    filter_taps = split_two(square[...].T[:channels, :tap_count])
+    copies[1].wait()
     tile = 128
     last = windows - 1
+    for b in range(1, windows):
+        ends[:, (b - 1) * tile : b * tile] = traces[:, b * HALF - tile : b * HALF]
     start = (last - 1) * HALF
-    before = [traces[:, start - tile : start]]
-    after = [traces[:, samples - tile :]]
-    edge = end_terms(filter_taps, tap_count, before, after)[0]
-    spectra[...] = dot_three(edge, table, tap_count - 1)
+    apart = traces[:, start - tile : start].astype(F32) - traces[:, samples - tile :].astype(F32)
+    edge = split_two(end_terms(taps[...], shifted, tap_count, apart))
     pieces = samples // PIECE
     x = jnp.concatenate([traces[:, q * PIECE : (q + 1) * PIECE] for q in range(pieces)], axis=0)
     turns = Turns()
-    for f in range(0, NF, CHUNK):
+    for i, f in enumerate(range(0, NF, CHUNK)):
         re = slice(f, f + CHUNK)
         im = slice(NF + f, NF + f + CHUNK)
+        copies[2 + 2 * i].wait()
+        copies[3 + 2 * i].wait()
+        pr = dot_three(filter_taps, table, tap_count, re)
+        pi = dot_three(filter_taps, table, tap_count, im)
+        response[:, re] = pr
+        response[:, im] = pi
         halves = half_spectra(x, table, channels, windows, turns, f)
-        pr, pi = response[:, re], response[:, im]
         for w in range(windows):
             xr, xi = halves[w]
             xr, xi = turns.sign * xr, turns.sign * xi
@@ -165,90 +193,96 @@
                 part[rows, re] = yr
                 part[rows, im] = yi
             else:
-                spectra[:, re] = spectra[:, re] + yr
-                spectra[:, im] = spectra[:, im] + yi
+                spectra[:, re] = yr + dot_three(edge, table, tap_count - 1, re)
+                spectra[:, im] = yi + dot_three(edge, table, tap_count - 1, im)
     whiten_all(spectra, white, channels)
 
 
-def picks_kernel(shape, where, counts, slots, *refs):
-    channels, windows, pairs, block_rows, chips, times = shape
-    wanted, picks, chosen = refs[:chips], refs[chips], refs[chips + 1]
+def mark_picks(shape, where, counts, slots, wanted, chosen):
+    channels, windows, pairs, block_rows, chips, _ = shape
     group = where[0]
     first = jnp.int32(0)
     for g in range(counts.shape[0]):
         first = first + jnp.where(g < group, counts[g], 0)
     owned = counts[group]
     width = windows * channels
-    column = lax.broadcasted_iota(jnp.int32, (1, width), 1) % channels
-    base = 2 * chips * block_rows
-    chosen[...] = jnp.zeros_like(chosen)
+    lane = lax.broadcasted_iota(jnp.int32, (1, width), 1)
+    columns = [jnp.where(lane // channels == w, lane % channels, -2) for w in range(windows)]
+    unused = block_rows - windows * pairs
     for core in range(2):
         for d in range(chips):
+            base = (core * chips + d) * block_rows
             for p in range(pairs):
                 slot = wanted[d][core, p] - first
                 mine = (slot >= 0) & (slot < owned)
                 channel = slots[group, jnp.where(mine, slot, 0)]
-                line = (column == jnp.where(mine, channel, -1)).astype(F32)
-                row = (core * chips + d) * block_rows + p
+                channel = jnp.where(mine, channel, -1)
                 for w in range(windows):
-                    chosen[row + w * pairs : row + w * pairs + 1, :] = line
-    block = lax.broadcasted_iota(jnp.int32, (block_rows, width), 0)
-    window = lax.broadcasted_iota(jnp.int32, (block_rows, width), 1) // channels
-    inside = (block >= window * pairs) & (block < (window + 1) * pairs)
-    for b in range(2 * chips):
-        rows = slice(b * block_rows, (b + 1) * block_rows)
-        picks[rows, :] = jnp.where(inside, chosen[rows, :], 0.0).astype(BF16)
-    part = channels // times
-    count = windows * channels
-    row = lax.broadcasted_iota(jnp.int32, (count, width), 0)
-    col = lax.broadcasted_iota(jnp.int32, (count, width), 1)
-    distance = row // (windows * part)
-    line = (where[1] ^ distance) * part + row % part
-    at = (row // part) % windows * channels + line
-    picks[base : base + count, :] = (col == at).astype(F32).astype(BF16)
-
-
-def rest_kernel(
-    shape, traces, halo, taps, table, part, own_white, response, picks, *refs
-):
-    channels, windows, pairs, block_rows, chips, times = shape
-    keep, send = refs[:2]
-    blocks = refs[2 : 2 + times]
-    square, spectra, white = refs[2 + times :]
+                    row = base + w * pairs + p
+                    chosen[row : row + 1, :] = (columns[w] == channel).astype(F32)
+            if unused:
+                chosen[base + windows * pairs : base + block_rows, :] = jnp.zeros(
+                    (unused, width), F32
+                )
+
+
+def rest_kernel(shape, where, counts, slots, *refs):
+    channels, windows, _, block_rows, chips, times = shape
+    wanted = refs[:chips]
+    halo, ends, taps, table, part, own_white, response = refs[chips : chips + 7]
+    keep, send = refs[chips + 7 : chips + 9]
+    blocks = refs[chips + 9 : chips + 9 + times]
+    shifted, spectra, white, chosen = refs[chips + 9 + times :]
     tap_count = taps.shape[0]
-    filter_taps = turned_taps(taps, square)
     tile = halo.shape[1] - HALF
+    rest = windows - 1
+
     before = [halo[:, :tile], halo[:, HALF:]]
-    for b in range(1, windows - 2):
-        before.append(traces[:, b * HALF - tile : b * HALF])
-    after = [traces[:, (w + 1) * HALF - tile : (w + 1) * HALF] for w in range(windows - 1)]
-    edges = end_terms(filter_taps, tap_count, before, after)
-    spectra[...] = part[...] + dot_three(jnp.concatenate(edges, axis=0), table, tap_count - 1)
+    before += [ends[:, (b - 1) * tile : b * tile] for b in range(1, windows - 2)]
+    after = [ends[:, w * tile : (w + 1) * tile] for w in range(rest)]
+    apart = jnp.concatenate([b.astype(F32) - a.astype(F32) for b, a in zip(before, after)], axis=0)
+    taps_wide = jnp.concatenate([taps[...]] * rest, axis=1)
+    edge = split_two(end_terms(taps_wide, shifted, tap_count, apart))
     x = jnp.concatenate(
         [halo[:, tile + q * PIECE : tile + (q + 1) * PIECE] for q in range(HALF // PIECE)],
         axis=0,
     )
+    mark_picks(shape, where, counts, slots, wanted, chosen)
     turns = Turns()
     for f in range(0, NF, CHUNK):
         re = slice(f, f + CHUNK)
         im = slice(NF + f, NF + f + CHUNK)
         xr, xi = half_spectra(x, table, channels, 1, turns, f)[0]
         pr, pi = response[:, re], response[:, im]
-        spectra[:channels, re] = spectra[:channels, re] + (xr * pr - xi * pi)
-        spectra[:channels, im] = spectra[:channels, im] + (xr * pi + xi * pr)
-    count = (windows - 1) * channels
+        er = dot_three(edge, table, tap_count - 1, re)
+        ei = dot_three(edge, table, tap_count - 1, im)
+        spectra[:channels, re] = part[:channels, re] + er[:channels] + (xr * pr - xi * pi)
+        spectra[:channels, im] = part[:channels, im] + ei[:channels] + (xr * pi + xi * pr)
+        spectra[channels:, re] = part[channels:, re] + er[channels:]
+        spectra[channels:, im] = part[channels:, im] + ei[channels:]
+    count = rest * channels
     whiten_all(spectra, white, count)
     white[count:, :] = own_white[...]
     base = 2 * chips * block_rows
-    rows = windows * channels // times
-    choose = picks[...]
+    size = channels // times
+    choose = chosen[...].astype(BF16)
     for f in range(0, 2 * NF, CHUNK):
         cols = slice(f, f + CHUNK)
         out = dot(choose, white[:, cols]).astype(BF16)
         keep[:, cols] = out[: base // 2]
-        send[:, cols] = out[base // 2 : base]
-        for d in range(times):
-            blocks[d][:, cols] = out[base + d * rows : base + (d + 1) * rows]
+        send[:, cols] = out[base // 2 :]
+    for d in range(times):
+        line = (where[1] ^ d) * size
+        for w in range(windows):
+            if size % ROWS == 0:
+                at = pl.multiple_of(w * channels + line, ROWS)
+                blocks[d][w * size : (w + 1) * size, :] = white[pl.ds(at, size), :]
+            else:
+                row = lax.broadcasted_iota(jnp.int32, (size, channels), 0)
+                col = lax.broadcasted_iota(jnp.int32, (size, channels), 1)
+                move = (col == row + line).astype(F32).astype(BF16)
+                moved = dot(move, white[w * channels : (w + 1) * channels, :])
+                blocks[d][w * size : (w + 1) * size, :] = moved.astype(BF16)
 
 
 def correlate_kernel(windows, factor, count, has_total, *refs):
@@ -275,7 +309,7 @@
             re = slice(f, f + 128)
             im = slice(NF + f, NF + f + 128)
             if has_total:
-                total_r, total_i = total[i, :, re], total[i, :, im]
+                total_r, total_i = total[start + i, :, re], total[start + i, :, im]
             else:
                 total_r = jnp.zeros((part, 128), F32)
                 total_i = jnp.zeros((part, 128), F32)
@@ -300,9 +334,7 @@
         functools.partial(correlate_kernel, windows, factor, count, len(extra)),
         out_shape=jax.ShapeDtypeStruct((pairs, part, width), F32),
         grid=(pairs // step,),
-        in_specs=[pl.BlockSpec(r.shape, lambda i: (0, 0, 0)) for r in receivers]
-        + [pl.BlockSpec(s.shape, lambda i: (0, 0)) for s in sources]
-        + [block] * len(extra),
+        in_specs=[pl.BlockSpec(memory_space=pltpu.VMEM)] * (2 * count + len(extra)),
         out_specs=block,
         scratch_shapes=[
             pltpu.VMEM((count * windows, part, width), F32),
@@ -331,7 +363,9 @@
     tail = traces[:, samples - HALF - 128 :]
     halo = lax.ppermute(tail, "tm", [(i - 1, i) for i in range(1, times)])
     both = jnp.concatenate([block_sources, across(block_sources, "chan", 1)], axis=0)
-    wanted = [both] + [across(both, "chan", 2 * d) for d in range(1, chips)]
+    wanted = [both]
+    for d in range(1, chips):
+        wanted.append(across(both, "chan", 2 * d))
     where = jnp.stack([lax.axis_index("chan"), lax.axis_index("tm")]).astype(jnp.int32)
 
     shape = (channels, windows, pairs, block_rows, chips, times)
@@ -339,45 +373,58 @@
     vmem = pl.BlockSpec(memory_space=pltpu.VMEM)
     params = pltpu.CompilerParams(vmem_limit_bytes=LIMIT)
     width = windows * channels
-    all_rows = 2 * chips * block_rows + width
     taps = filter_taps.T
     table = jnp.asarray(piece_table())
-    part_spectra, own_white, response = pl.pallas_call(
+    own = pl.pallas_call(
         functools.partial(own_kernel, windows),
         out_shape=[
             jax.ShapeDtypeStruct((width - channels, 2 * NF), F32),
             jax.ShapeDtypeStruct((channels, 2 * NF), BF16),
             jax.ShapeDtypeStruct((channels, 2 * NF), F32),
+            jax.ShapeDtypeStruct((channels, (windows - 1) * 128), BF16),
+            jax.ShapeDtypeStruct(taps.shape, F32),
+            jax.ShapeDtypeStruct(table.shape, BF16),
         ],
-        in_specs=[vmem] * 3,
-        out_specs=[vmem] * 3,
-        scratch_shapes=[pltpu.VMEM((128, 128), F32), pltpu.VMEM((channels, 2 * NF), F32)],
+        in_specs=[pl.BlockSpec(memory_space=pltpu.HBM)] * 3,
+        out_specs=[vmem] * 6,
+        scratch_shapes=[
+            pltpu.VMEM(traces.shape, BF16),
+            pltpu.VMEM((128, 128), F32),
+            pltpu.VMEM((2 * tap_count + 6, channels), F32),
+            pltpu.VMEM((channels, 2 * NF), F32),
+            pltpu.SemaphoreType.DMA((2 + 2 * NF // CHUNK,)),
+        ],
         compiler_params=params,
         name="own",
-    )(traces, taps, table)
-    picks = pl.pallas_call(
-        functools.partial(picks_kernel, shape),
-        out_shape=jax.ShapeDtypeStruct((all_rows, width), BF16),
-        in_specs=[smem] * (3 + chips),
-        out_specs=vmem,
-        scratch_shapes=[pltpu.VMEM((2 * chips * block_rows, width), F32)],
-        compiler_params=params,
-        name="picks",
-    )(where, source_counts, source_channel, *wanted)
+    )(*(pltpu.with_memory_space_constraint(a, pltpu.HBM) for a in (traces, taps, table)))
+    part_spectra, own_white, response, ends, taps, table = own
     outs = pl.pallas_call(
         functools.partial(rest_kernel, shape),
         out_shape=[jax.ShapeDtypeStruct((chips * block_rows, 2 * NF), BF16)] * 2
         + [jax.ShapeDtypeStruct((windows * part, 2 * NF), BF16)] * times,
-        in_specs=[vmem] * 8,
+        in_specs=[smem] * (3 + chips) + [vmem] * 7,
         out_specs=[vmem] * (2 + times),
         scratch_shapes=[
-            pltpu.VMEM((128, 128), F32),
+            pltpu.VMEM((2 * tap_count + 6, width - channels), F32),
             pltpu.VMEM((width - channels, 2 * NF), F32),
             pltpu.VMEM((width, 2 * NF), BF16),
+            pltpu.VMEM((2 * chips * block_rows, width), F32),
         ],
         compiler_params=params,
         name="rest",
-    )(traces, halo, taps, table, part_spectra, own_white, response, picks)
+    )(
+        where,
+        source_counts,
+        source_channel,
+        *wanted,
+        halo,
+        ends,
+        taps,
+        table,
+        part_spectra,
+        own_white,
+        response,
+    )
     keep, send, blocks = outs[0], outs[1], outs[2:]
     gathered = keep + across(send, "chan", 1)
     pieces = [gathered[d * block_rows : (d + 1) * block_rows] for d in range(chips)]

time: 46.7 us -> 41.8 us (0.90)
  local copies, waits for them, and re-layouts: 4.46 us -> 1.05 us
  Pallas kernels: 11.8 us -> 10.6 us
    unnamed x14 -> x6, local copies, waits for them, and re-layouts: 3.47 us -> 0.01 us
    pallas_call x1 -> x0, Pallas kernels: 1.14 us -> none  [shards(): pl.pallas_call(functools.partial(picks_kernel, shape), out_shape=jax.Shap...]
    pallas_call x1, Pallas kernels: 3.67 us -> 3.01 us  [shards(): pl.pallas_call(functools.partial(rest_kernel, shape), out_shape=[jax.Shap...]
    pallas_call x1, Pallas kernels: 3.48 us -> 4.11 us  [shards(): pl.pallas_call(functools.partial(own_kernel, windows), out_shape=[jax.Sha...]
where the time goes in v3:
time: 41.8 us; the launch traced here: 41.6 us
  waiting for transfers between devices  16.5 us (39%)
  starting transfers between devices  13.1 us (31%)
  Pallas kernels  10.6 us (25%)
  local copies, waits for them, and re-layouts  1.05 us (3%)
    ppermute x10, waiting for transfers between devices, across(): return lax.ppermute(x, axis, [(i, i ^ distance) for i in range(size)])  16.5 us
    ppermute x10, starting transfers between devices, across(): return lax.ppermute(x, axis, [(i, i ^ distance) for i in range(size)])  8.22 us
    ppermute x1, starting transfers between devices, shards(): halo = lax.ppermute(tail, 'tm', [(i - 1, i) for i in range(1, times)])  4.89 us
    pallas_call x1, Pallas kernels, shards(): pl.pallas_call(functools.partial(own_kernel, windows), out_shape=[jax.Sha...  4.11 us
    pallas_call x2, Pallas kernels, correlate(): pl.pallas_call(functools.partial(correlate_kernel, windows, factor, count...  3.52 us
    pallas_call x1, Pallas kernels, shards(): pl.pallas_call(functools.partial(rest_kernel, shape), out_shape=[jax.Shap...  3.01 us
    slice x1, local copies, waits for them, and re-layouts, shards(): tail = traces[:, samples - HALF - 128:]  1.02 us
  transfers between devices with their start and end apart: 11, of which 7 were waited for; matrix products, arithmetic and copies ran while one was open for 0% of the time, Pallas kernels for 12%

profile of v3, /device:TPU:0, one launch (start us, length us, event | category | flops | bytes accessed | tf_op | source)
XLA Modules:
  0.0 41.6 jit_solution(2417675348867806603)
XLA Ops:
  0.0 0.0 copy-start.2
  0.0 0.0 copy-start
  0.0 0.0 copy-start.1
  0.0 1.0 %slice.15 = bf16[64,2176]{1,0:T(8,128)(2,1)S(1)} slice(bf16[64,6144]{1,0:T(8,128)(2,1)} %traces_in.1), slice={[0:64], [3968:6144]} | slice | bytes 557056 | tf_op jit(solution)/shard_map/slice | solution.py:363
  1.0 4.9 %collective-permute-start.4 = (bf16[64,2176]{1,0:T(8,128)(2,1)S(1)}, bf16[64,2176]{1,0:T(8,128)(2,1)S(1)}, u32[]{:S(2)}, u32[]{:S(2)}) collective-permute-start(bf16[64,2176]{1,0:T(8,128)(2,1)S(1)} %slice.15), channel_id=1, source_target_pairs={{0,1},{2,3},{4,5},{6,7},{8,9},{10,11},{12,13},{14,15},{16,17},{18,... | collective-permute-start | bytes 835592 | tf_op jit(solution)/shard_map/ppermute | solution.py:364
  5.9 0.1 collective-permute-start
  6.0 4.1 %own.1 = (f32[128,1024]{1,0:T(8,128)S(1)}, bf16[64,1024]{1,0:T(8,128)(2,1)S(1)}, f32[64,1024]{1,0:T(8,128)S(1)}, bf16[64,256]{1,0:T(8,128)(2,1)S(1)}, f32[33,64]...) custom-call(bf16[64,6144]{1,0:T(8,128)(2,1)} %traces_in.1, f32[33,64]{1,0:T(8,128)} %bitcast.8, ...), custom_call_target="tpu_custom_call" | custom-call | tf_op jit(solution)/shard_map/own/pallas_call | solution.py:378
  10.1 0.1 pad_add_fusion.1.where
  10.2 0.0 collective-permute-done
  10.2 0.0 copy-done.2
  10.2 3.7 %collective-permute-start.3 = (s32[2,12]{1,0:T(2,128)S(1)}, s32[2,12]{1,0:T(2,128)S(1)}, u32[]{:S(2)}, u32[]{:S(2)}) collective-permute-start(s32[2,12]{1,0:T(2,128)S(1)} %pad_add_fusion.refs_0_), channel_id=1, source_target_pairs={{0,12},{2,14},{4,8},{6,10},{8,4},{10,6},{12,0},{14,2},{1,13},{3,15... | collective-permute-start | bytes 296 | tf_op jit(solution)/shard_map/ppermute | solution.py:361
  13.9 0.0 collective-permute-start.2
  13.9 0.8 %collective-permute-start.1 = (s32[2,12]{1,0:T(2,128)S(1)}, s32[2,12]{1,0:T(2,128)S(1)}, u32[]{:S(2)}, u32[]{:S(2)}) collective-permute-start(s32[2,12]{1,0:T(2,128)S(1)} %pad_add_fusion.refs_0_), channel_id=1, source_target_pairs={{0,4},{2,6},{4,0},{6,2},{8,12},{10,14},{12,8},{14,10},{1,5},{3,7},... | collective-permute-start | bytes 296 | tf_op jit(solution)/shard_map/ppermute | solution.py:361
  14.7 1.0 %collective-permute-done.3.refs_3_ = s32[2,12]{1,0:T(2,128)S(1)} collective-permute-done((s32[2,12]{1,0:T(2,128)S(1)}, s32[2,12]{1,0:T(2,128)S(1)}, u32[]{:S(2)}, u32[]{:S(2)}) %collective-permute-start.3) | collective-permute-done | bytes 128 | tf_op jit(solution)/shard_map/ppermute | solution.py:361
  15.7 2.7 %collective-permute-done.2.refs_2_ = s32[2,12]{1,0:T(2,128)S(1)} collective-permute-done((s32[2,12]{1,0:T(2,128)S(1)}, s32[2,12]{1,0:T(2,128)S(1)}, u32[]{:S(2)}, u32[]{:S(2)}) %collective-permute-start.2) | collective-permute-done | bytes 128 | tf_op jit(solution)/shard_map/ppermute | solution.py:361
  18.4 0.0 collective-permute-done.1.refs_1_
  18.4 0.0 collective-permute-done.4.refs_4_
  18.4 0.0 copy-done
  18.4 0.0 copy-done.1
  18.4 3.0 %rest.1 = (bf16[160,1024]{1,0:T(8,128)(2,1)S(1)}, bf16[160,1024]{1,0:T(8,128)(2,1)S(1)}, bf16[96,1024]{1,0:T(8,128)(2,1)S(1)}, bf16[96,1024]{1,0:T(8,128)(2,1)S(1)}) custom-call(s32[2]{0:T(128)S(1)} %pad_add_fusion.1.where, s32[8]{0:T(128)S(1)} %copy-done.1, s32[8,36]{1,0:T(8,128)S(1)} %copy-done, s32[2,12]{1,0:T(2,128)S(1)} %pad_add_fusion.refs_0_, ...), custom_call_target="tpu_custom_call" | custom-call | tf_op jit(solution)/shard_map/rest/pallas_call | solution.py:401
  21.4 0.1 collective-permute-start.6
  21.5 1.6 %collective-permute-done.6 = bf16[160,1024]{1,0:T(8,128)(2,1)S(1)} collective-permute-done((bf16[160,1024]{1,0:T(8,128)(2,1)S(1)}, bf16[160,1024]{1,0:T(8,128)(2,1)S(1)}, u32[]{:S(2)}, u32[]{:S(2)}) %collective-permute-start.6) | collective-permute-done | bytes 327712 | tf_op jit(solution)/shard_map/ppermute | solution.py:361
  23.1 0.1 add.12
  23.2 0.1 collective-permute-start.7
  23.3 3.5 %collective-permute-start.9 = (bf16[40,1024]{1,0:T(8,128)(2,1)S(1)}, bf16[40,1024]{1,0:T(8,128)(2,1)S(1)}, u32[]{:S(2)}, u32[]{:S(2)}) collective-permute-start(bf16[40,1024]{1,0:T(8,128)(2,1)S(1)} %get-tuple-element.26), channel_id=1, source_target_pairs={{0,12},{2,14},{4,8},{6,10},{8,4},{10,6},{12,0},{14,2},{1,13},{3,15... | collective-permute-start | bytes 245768 | tf_op jit(solution)/shard_map/ppermute | solution.py:361
  26.8 0.0 collective-permute-start.8
  26.8 0.0 collective-permute-start.5
  26.8 1.0 %collective-permute-done.7 = bf16[40,1024]{1,0:T(8,128)(2,1)S(1)} collective-permute-done((bf16[40,1024]{1,0:T(8,128)(2,1)S(1)}, bf16[40,1024]{1,0:T(8,128)(2,1)S(1)}, u32[]{:S(2)}, u32[]{:S(2)}) %collective-permute-start.7) | collective-permute-done | bytes 81952 | tf_op jit(solution)/shard_map/ppermute | solution.py:361
  27.8 4.1 %collective-permute-done.9 = bf16[40,1024]{1,0:T(8,128)(2,1)S(1)} collective-permute-done((bf16[40,1024]{1,0:T(8,128)(2,1)S(1)}, bf16[40,1024]{1,0:T(8,128)(2,1)S(1)}, u32[]{:S(2)}, u32[]{:S(2)}) %collective-permute-start.9) | collective-permute-done | bytes 81952 | tf_op jit(solution)/shard_map/ppermute | solution.py:361
  31.9 2.6 %collective-permute-done.8 = bf16[40,1024]{1,0:T(8,128)(2,1)S(1)} collective-permute-done((bf16[40,1024]{1,0:T(8,128)(2,1)S(1)}, bf16[40,1024]{1,0:T(8,128)(2,1)S(1)}, u32[]{:S(2)}, u32[]{:S(2)}) %collective-permute-start.8) | collective-permute-done | bytes 81952 | tf_op jit(solution)/shard_map/ppermute | solution.py:361
  34.5 0.1 collective-permute-start.10
  34.6 0.9 %correlate.2.refs_2_ = f32[12,32,1024]{2,1,0:T(8,128)S(1)} custom-call(bf16[3,32,1024]{2,1,0:T(8,128)(2,1)S(1)} %bitcast.6, bf16[40,1024]{1,0:T(8,128)(2,1)S(1)} %fusion.1.refs_1_), custom_call_target="tpu_custom_call" | custom-call | tf_op jit(solution)/shard_map/correlate/pallas_call | solution.py:333
  35.4 0.0 collective-permute-done.5
  35.5 3.5 %collective-permute-done.10.refs_1_ = bf16[40,1024]{1,0:T(8,128)(2,1)S(1)} collective-permute-done((bf16[40,1024]{1,0:T(8,128)(2,1)S(1)}, bf16[40,1024]{1,0:T(8,128)(2,1)S(1)}, u32[]{:S(2)}, u32[]{:S(2)}) %collective-permute-start.10) | collective-permute-done | bytes 81952 | tf_op jit(solution)/shard_map/ppermute | solution.py:361
  39.0 2.6 %correlate.3 = f32[12,32,1024]{2,1,0:T(8,128)} custom-call(bf16[3,32,1024]{2,1,0:T(8,128)(2,1)S(1)} %bitcast.7, bf16[40,1024]{1,0:T(8,128)(2,1)S(1)} %collective-permute-done.10.refs_1_, f32[12,32,1024]{2,1,0:T(8,128)S(1)} %correlate.2.refs_2_), custom_call_target="tpu_custom_call" | custom-call | tf_op jit(solution)/shard_map/correlate/pallas_call | solution.py:333
  (3 shorter events, 0.0 us)
Async XLA Ops:
  0.0 10.2 %copy-start.2 = (s32[1,12]{1,0:T(1,128)S(1)}, s32[1,12]{1,0:T(1,128)}, u32[]{:S(2)}) copy-start(s32[1,12]{1,0:T(1,128)} %param.10) | copy-start | bytes 148
  0.0 18.4 %copy-start = (s32[8,36]{1,0:T(8,128)S(1)}, s32[8,36]{1,0:T(8,128)}, u32[]{:S(2)}) copy-start(s32[8,36]{1,0:T(8,128)} %slots.1) | copy-start | bytes 3460
  0.0 18.4 %copy-start.1 = (s32[8]{0:T(128)S(1)}, s32[8]{0:T(128)}, u32[]{:S(2)}) copy-start(s32[8]{0:T(128)} %counts.1) | copy-start | bytes 100
  1.0 17.3 %collective-permute-start.4 = (bf16[64,2176]{1,0:T(8,128)(2,1)S(1)}, bf16[64,2176]{1,0:T(8,128)(2,1)S(1)}, u32[]{:S(2)}, u32[]{:S(2)}) collective-permute-start(bf16[64,2176]{1,0:T(8,128)(2,1)S(1)} %slice.15), channel_id=1, source_target_pairs={{0,1},{2,3},{4,5},{6,7},{8,9},{10,11},{12,13},{14,15},{16,17},{18,... | collective-permute-start | bytes 835592 | tf_op jit(solution)/shard_map/ppermute | solution.py:364
  5.9 4.3 %collective-permute-start = (s32[1,12]{1,0:T(1,128)}, s32[1,12]{1,0:T(1,128)S(1)}, u32[]{:S(2)}, u32[]{:S(2)}) collective-permute-start(s32[1,12]{1,0:T(1,128)} %param.10), channel_id=1, source_target_pairs={{0,2},{2,0},{4,6},{6,4},{8,10},{10,8},{12,14},{14,12},{1,3},{3,1},... | collective-permute-start | bytes 152 | tf_op jit(solution)/shard_map/ppermute | solution.py:361
  10.2 5.4 %collective-permute-start.3 = (s32[2,12]{1,0:T(2,128)S(1)}, s32[2,12]{1,0:T(2,128)S(1)}, u32[]{:S(2)}, u32[]{:S(2)}) collective-permute-start(s32[2,12]{1,0:T(2,128)S(1)} %pad_add_fusion.refs_0_), channel_id=1, source_target_pairs={{0,12},{2,14},{4,8},{6,10},{8,4},{10,6},{12,0},{14,2},{1,13},{3,15... | collective-permute-start | bytes 296 | tf_op jit(solution)/shard_map/ppermute | solution.py:361
  13.9 4.5 %collective-permute-start.2 = (s32[2,12]{1,0:T(2,128)S(1)}, s32[2,12]{1,0:T(2,128)S(1)}, u32[]{:S(2)}, u32[]{:S(2)}) collective-permute-start(s32[2,12]{1,0:T(2,128)S(1)} %pad_add_fusion.refs_0_), channel_id=1, source_target_pairs={{0,8},{2,10},{4,12},{6,14},{8,0},{10,2},{12,4},{14,6},{1,9},{3,11}... | collective-permute-start | bytes 296 | tf_op jit(solution)/shard_map/ppermute | solution.py:361
  13.9 4.5 %collective-permute-start.1 = (s32[2,12]{1,0:T(2,128)S(1)}, s32[2,12]{1,0:T(2,128)S(1)}, u32[]{:S(2)}, u32[]{:S(2)}) collective-permute-start(s32[2,12]{1,0:T(2,128)S(1)} %pad_add_fusion.refs_0_), channel_id=1, source_target_pairs={{0,4},{2,6},{4,0},{6,2},{8,12},{10,14},{12,8},{14,10},{1,5},{3,7},... | collective-permute-start | bytes 296 | tf_op jit(solution)/shard_map/ppermute | solution.py:361
  21.4 1.7 %collective-permute-start.6 = (bf16[160,1024]{1,0:T(8,128)(2,1)S(1)}, bf16[160,1024]{1,0:T(8,128)(2,1)S(1)}, u32[]{:S(2)}, u32[]{:S(2)}) collective-permute-start(bf16[160,1024]{1,0:T(8,128)(2,1)S(1)} %get-tuple-element.23), channel_id=1, source_target_pairs={{0,2},{2,0},{4,6},{6,4},{8,10},{10,8},{12,14},{14,12},{1,3},{3,1},... | collective-permute-start | bytes 983048 | tf_op jit(solution)/shard_map/ppermute | solution.py:361
  23.2 4.6 %collective-permute-start.7 = (bf16[40,1024]{1,0:T(8,128)(2,1)S(1)}, bf16[40,1024]{1,0:T(8,128)(2,1)S(1)}, u32[]{:S(2)}, u32[]{:S(2)}) collective-permute-start(bf16[40,1024]{1,0:T(8,128)(2,1)S(1)} %get-tuple-element.25), channel_id=1, source_target_pairs={{0,4},{2,6},{4,0},{6,2},{8,12},{10,14},{12,8},{14,10},{1,5},{3,7},... | collective-permute-start | bytes 245768 | tf_op jit(solution)/shard_map/ppermute | solution.py:361
  23.3 8.6 %collective-permute-start.9 = (bf16[40,1024]{1,0:T(8,128)(2,1)S(1)}, bf16[40,1024]{1,0:T(8,128)(2,1)S(1)}, u32[]{:S(2)}, u32[]{:S(2)}) collective-permute-start(bf16[40,1024]{1,0:T(8,128)(2,1)S(1)} %get-tuple-element.26), channel_id=1, source_target_pairs={{0,12},{2,14},{4,8},{6,10},{8,4},{10,6},{12,0},{14,2},{1,13},{3,15... | collective-permute-start | bytes 245768 | tf_op jit(solution)/shard_map/ppermute | solution.py:361
  26.8 7.7 %collective-permute-start.8 = (bf16[40,1024]{1,0:T(8,128)(2,1)S(1)}, bf16[40,1024]{1,0:T(8,128)(2,1)S(1)}, u32[]{:S(2)}, u32[]{:S(2)}) collective-permute-start(bf16[40,1024]{1,0:T(8,128)(2,1)S(1)} %get-tuple-element.27), channel_id=1, source_target_pairs={{0,8},{2,10},{4,12},{6,14},{8,0},{10,2},{12,4},{14,6},{1,9},{3,11}... | collective-permute-start | bytes 245768 | tf_op jit(solution)/shard_map/ppermute | solution.py:361
  26.8 8.7 %collective-permute-start.5 = (bf16[96,1024]{1,0:T(8,128)(2,1)S(1)}, bf16[96,1024]{1,0:T(8,128)(2,1)S(1)}, u32[]{:S(2)}, u32[]{:S(2)}) collective-permute-start(bf16[96,1024]{1,0:T(8,128)(2,1)S(1)} %get-tuple-element.21), channel_id=1, source_target_pairs={{0,1},{1,0},{2,3},{3,2},{4,5},{5,4},{6,7},{7,6},{8,9},{9,8},{10,11... | collective-permute-start | bytes 589832 | tf_op jit(solution)/shard_map/ppermute | solution.py:361
  34.5 4.5 %collective-permute-start.10 = (bf16[40,1024]{1,0:T(8,128)(2,1)S(1)}, bf16[40,1024]{1,0:T(8,128)(2,1)S(1)}, u32[]{:S(2)}, u32[]{:S(2)}) collective-permute-start(bf16[40,1024]{1,0:T(8,128)(2,1)S(1)} %fusion.1.refs_1_), channel_id=1, source_target_pairs={{0,1},{1,0},{2,3},{3,2},{4,5},{5,4},{6,7},{7,6},{8,9},{9,8},{10,11... | collective-permute-start | bytes 245768 | tf_op jit(solution)/shard_map/ppermute | solution.py:361

commit v4 on v3

--- a/solution.py
+++ b/solution.py
@@ -125,42 +125,26 @@
     lax.fori_loop(0, count // ROWS, step, 0, unroll=2)
 
 
-def own_kernel(
-    windows,
-    traces_in,
-    taps_in,
-    table_in,
-    part,
-    white,
-    response,
-    ends,
-    taps,
-    table,
-    traces,
-    square,
-    shifted,
-    spectra,
-    sems,
-):
+def head_kernel(traces_in, taps_in, table_in, tail, traces, taps, table, sems):
+    start = traces.shape[1] - tail.shape[1]
+    copies = [
+        pltpu.make_async_copy(traces_in.at[:, start:], tail, sems.at[0]),
+        pltpu.make_async_copy(traces_in, traces, sems.at[1]),
+        pltpu.make_async_copy(taps_in, taps, sems.at[2]),
+        pltpu.make_async_copy(table_in, table, sems.at[3]),
+    ]
+    for copy in copies:
+        copy.start()
+    for copy in copies:
+        copy.wait()
+
+
+def own_kernel(windows, traces, taps, table, part, white, response, ends, square, shifted, spectra):
     channels, samples = traces.shape
     tap_count = taps.shape[0]
-    copies = [
-        pltpu.make_async_copy(taps_in, taps, sems.at[0]),
-        pltpu.make_async_copy(traces_in, traces, sems.at[1]),
-    ]
-    order = [c for f in range(0, NF, CHUNK) for c in (f, NF + f)]
-    for i, c in enumerate(order):
-        cols = slice(c, c + CHUNK)
-        copies.append(
-            pltpu.make_async_copy(table_in.at[:, cols], table.at[:, cols], sems.at[2 + i])
-        )
-    for copy in copies:
-        copy.start()
-    copies[0].wait()
     square[...] = jnp.zeros_like(square)
     square[:tap_count, :channels] = taps[...]
     filter_taps = split_two(square[...].T[:channels, :tap_count])
-    copies[1].wait()
     tile = 128
     last = windows - 1
     for b in range(1, windows):
@@ -171,11 +155,9 @@
     pieces = samples // PIECE
     x = jnp.concatenate([traces[:, q * PIECE : (q + 1) * PIECE] for q in range(pieces)], axis=0)
     turns = Turns()
-    for i, f in enumerate(range(0, NF, CHUNK)):
+    for f in range(0, NF, CHUNK):
         re = slice(f, f + CHUNK)
         im = slice(NF + f, NF + f + CHUNK)
-        copies[2 + 2 * i].wait()
-        copies[3 + 2 * i].wait()
         pr = dot_three(filter_taps, table, tap_count, re)
         pi = dot_three(filter_taps, table, tap_count, im)
         response[:, re] = pr
@@ -209,11 +191,12 @@
     lane = lax.broadcasted_iota(jnp.int32, (1, width), 1)
     columns = [jnp.where(lane // channels == w, lane % channels, -2) for w in range(windows)]
     unused = block_rows - windows * pairs
+    per = wanted[0].shape[0]
     for core in range(2):
         for d in range(chips):
             base = (core * chips + d) * block_rows
             for p in range(pairs):
-                slot = wanted[d][core, p] - first
+                slot = wanted[2 * d // per][(2 * d + core) % per, p] - first
                 mine = (slot >= 0) & (slot < owned)
                 channel = slots[group, jnp.where(mine, slot, 0)]
                 channel = jnp.where(mine, channel, -1)
@@ -228,11 +211,12 @@
 
 def rest_kernel(shape, where, counts, slots, *refs):
     channels, windows, _, block_rows, chips, times = shape
-    wanted = refs[:chips]
-    halo, ends, taps, table, part, own_white, response = refs[chips : chips + 7]
-    keep, send = refs[chips + 7 : chips + 9]
-    blocks = refs[chips + 9 : chips + 9 + times]
-    shifted, spectra, white, chosen = refs[chips + 9 + times :]
+    wanted = refs[:2] if chips > 1 else refs[:1]
+    refs = refs[len(wanted) :]
+    halo, ends, taps, table, part, own_white, response = refs[:7]
+    keep, send = refs[7:9]
+    blocks = refs[9 : 9 + times]
+    shifted, spectra, white, chosen = refs[9 + times :]
     tap_count = taps.shape[0]
     tile = halo.shape[1] - HALF
     rest = windows - 1
@@ -285,64 +269,74 @@
                 blocks[d][w * size : (w + 1) * size, :] = moved.astype(BF16)
 
 
-def correlate_kernel(windows, factor, count, has_total, *refs):
+def correlate_kernel(windows, factor, count, *refs):
     receivers = refs[:count]
     sources = refs[count : 2 * count]
-    total = refs[2 * count] if has_total else None
-    out, line_r, line_s = refs[2 * count + has_total :]
-    step, part = out.shape[0], out.shape[1]
-    pairs = line_s.shape[0]
-
-    @pl.when(pl.program_id(0) == 0)
-    def _():
-        for d in range(count):
-            for w in range(windows):
-                at = d * windows + w
-                line_r[at] = receivers[d][w].astype(F32) * factor
-                rows = sources[d][w * pairs : (w + 1) * pairs, :].astype(F32)
-                for p in range(pairs):
-                    line_s[p, at : at + 1, :] = rows[p : p + 1, :]
-
-    start = pl.program_id(0) * step
-    for i in range(step):
+    last = len(refs) == 2 * count + 6
+    total = refs[2 * count] if last else None
+    out, line_r, line_s = refs[2 * count + last : 2 * count + last + 3]
+    held, sems = refs[-2:] if last else (out, None)
+    pairs, part = out.shape[0], out.shape[1]
+    for d in range(count):
+        for w in range(windows):
+            at = d * windows + w
+            line_r[at] = receivers[d][w].astype(F32) * factor
+            rows = sources[d][w * pairs : (w + 1) * pairs, :].astype(F32)
+            for p in range(pairs):
+                line_s[p, at : at + 1, :] = rows[p : p + 1, :]
+
+    def copy(p):
+        return pltpu.make_async_copy(held.at[p], out.at[p], sems.at[p])
+
+    def one(p, carry):
         for f in range(0, NF, 128):
             re = slice(f, f + 128)
             im = slice(NF + f, NF + f + 128)
-            if has_total:
-                total_r, total_i = total[start + i, :, re], total[start + i, :, im]
+            if last:
+                total_r, total_i = total[p, :, re], total[p, :, im]
             else:
                 total_r = jnp.zeros((part, 128), F32)
                 total_i = jnp.zeros((part, 128), F32)
             for at in range(count * windows):
                 rr = line_r[at, :, re]
                 ri = line_r[at, :, im]
-                sr = line_s[start + i, at : at + 1, re]
-                si = line_s[start + i, at : at + 1, im]
+                sr = line_s[p, at : at + 1, re]
+                si = line_s[p, at : at + 1, im]
                 total_r = total_r + (sr * rr + si * ri)
                 total_i = total_i + (sr * ri - si * rr)
-            out[i, :, re] = total_r
-            out[i, :, im] = total_i
+            held[p, :, re] = total_r
+            held[p, :, im] = total_i
+        if last:
+            copy(p).start()
+        return carry
+
+    lax.fori_loop(0, pairs, one, 0)
+    if last:
+        for p in range(pairs):
+            copy(p).wait()
 
 
 def correlate(receivers, sources, total, pairs, factor):
     windows, part, width = receivers[0].shape
     count = len(receivers)
-    step = next(s for s in (2, 1) if pairs % s == 0)
-    block = pl.BlockSpec((step, part, width), lambda i: (i, 0, 0))
-    extra = [] if total is None else [total]
+    vmem = pl.BlockSpec(memory_space=pltpu.VMEM)
+    shape = (pairs, part, width)
+    last = total is not None
+    scratch = [
+        pltpu.VMEM((count * windows, part, width), F32),
+        pltpu.VMEM((pairs, -(-count * windows // 8) * 8, width), F32),
+    ]
+    if last:
+        scratch += [pltpu.VMEM(shape, F32), pltpu.SemaphoreType.DMA((pairs,))]
     return pl.pallas_call(
-        functools.partial(correlate_kernel, windows, factor, count, len(extra)),
-        out_shape=jax.ShapeDtypeStruct((pairs, part, width), F32),
-        grid=(pairs // step,),
-        in_specs=[pl.BlockSpec(memory_space=pltpu.VMEM)] * (2 * count + len(extra)),
-        out_specs=block,
-        scratch_shapes=[
-            pltpu.VMEM((count * windows, part, width), F32),
-            pltpu.VMEM((pairs, -(-count * windows // 8) * 8, width), F32),
-        ],
+        functools.partial(correlate_kernel, windows, factor, count),
+        out_shape=jax.ShapeDtypeStruct(shape, F32),
+        in_specs=[vmem] * (2 * count + last),
+        out_specs=pl.BlockSpec(memory_space=pltpu.HBM) if last else vmem,
+        scratch_shapes=scratch,
         compiler_params=pltpu.CompilerParams(vmem_limit_bytes=LIMIT),
         name="correlate",
-    )(*receivers, *sources, *extra)
+    )(*receivers, *sources, *([total] if last else []))
 
 
 def shards(traces, filter_taps, source_counts, source_channel, block_sources):
@@ -360,21 +354,33 @@
         size = lax.axis_size(axis)
         return lax.ppermute(x, axis, [(i, i ^ distance) for i in range(size)])
 
-    tail = traces[:, samples - HALF - 128 :]
-    halo = lax.ppermute(tail, "tm", [(i - 1, i) for i in range(1, times)])
-    both = jnp.concatenate([block_sources, across(block_sources, "chan", 1)], axis=0)
-    wanted = [both]
-    for d in range(1, chips):
-        wanted.append(across(both, "chan", 2 * d))
-    where = jnp.stack([lax.axis_index("chan"), lax.axis_index("tm")]).astype(jnp.int32)
-
-    shape = (channels, windows, pairs, block_rows, chips, times)
     smem = pl.BlockSpec(memory_space=pltpu.SMEM)
     vmem = pl.BlockSpec(memory_space=pltpu.VMEM)
+    hbm = pl.BlockSpec(memory_space=pltpu.HBM)
     params = pltpu.CompilerParams(vmem_limit_bytes=LIMIT)
+    bits = [1 << b for b in range(chips.bit_length() - 1)]
+
+    other = across(block_sources, "chan", 1)
+    inputs = (traces, filter_taps.T, jnp.asarray(piece_table()))
+    tail, traces, taps, table = pl.pallas_call(
+        head_kernel,
+        out_shape=[jax.ShapeDtypeStruct((channels, HALF + 128), BF16)]
+        + [jax.ShapeDtypeStruct(a.shape, a.dtype) for a in inputs],
+        in_specs=[hbm] * 3,
+        out_specs=[vmem] * 4,
+        scratch_shapes=[pltpu.SemaphoreType.DMA((4,))],
+        compiler_params=params,
+        name="head",
+    )(*(pltpu.with_memory_space_constraint(a, pltpu.HBM) for a in inputs))
+    halo = lax.ppermute(tail, "tm", [(i - 1, i) for i in range(1, times)])
+    wanted = [jnp.concatenate([block_sources, other], axis=0)]
+    for bit in bits:
+        known = jnp.concatenate(wanted, axis=0)
+        wanted = [known, across(known, "chan", 2 * bit)]
+    where = jnp.stack([lax.axis_index("chan"), lax.axis_index("tm")]).astype(jnp.int32)
+
+    shape = (channels, windows, pairs, block_rows, chips, times)
     width = windows * channels
-    taps = filter_taps.T
-    table = jnp.asarray(piece_table())
     own = pl.pallas_call(
         functools.partial(own_kernel, windows),
         out_shape=[
@@ -382,27 +388,23 @@
             jax.ShapeDtypeStruct((channels, 2 * NF), BF16),
             jax.ShapeDtypeStruct((channels, 2 * NF), F32),
             jax.ShapeDtypeStruct((channels, (windows - 1) * 128), BF16),
-            jax.ShapeDtypeStruct(taps.shape, F32),
-            jax.ShapeDtypeStruct(table.shape, BF16),
         ],
-        in_specs=[pl.BlockSpec(memory_space=pltpu.HBM)] * 3,
-        out_specs=[vmem] * 6,
+        in_specs=[vmem] * 3,
+        out_specs=[vmem] * 4,
         scratch_shapes=[
-            pltpu.VMEM(traces.shape, BF16),
             pltpu.VMEM((128, 128), F32),
             pltpu.VMEM((2 * tap_count + 6, channels), F32),
             pltpu.VMEM((channels, 2 * NF), F32),
-            pltpu.SemaphoreType.DMA((2 + 2 * NF // CHUNK,)),
         ],
         compiler_params=params,
         name="own",
-    )(*(pltpu.with_memory_space_constraint(a, pltpu.HBM) for a in (traces, taps, table)))
-    part_spectra, own_white, response, ends, taps, table = own
+    )(traces, taps, table)
+    part_spectra, own_white, response, ends = own
     outs = pl.pallas_call(
         functools.partial(rest_kernel, shape),
         out_shape=[jax.ShapeDtypeStruct((chips * block_rows, 2 * NF), BF16)] * 2
         + [jax.ShapeDtypeStruct((windows * part, 2 * NF), BF16)] * times,
-        in_specs=[smem] * (3 + chips) + [vmem] * 7,
+        in_specs=[smem] * (3 + len(wanted)) + [vmem] * 7,
         out_specs=[vmem] * (2 + times),
         scratch_shapes=[
             pltpu.VMEM((2 * tap_count + 6, width - channels), F32),
@@ -428,10 +430,20 @@
     keep, send, blocks = outs[0], outs[1], outs[2:]
     gathered = keep + across(send, "chan", 1)
     pieces = [gathered[d * block_rows : (d + 1) * block_rows] for d in range(chips)]
+    for bit in bits:
+        onward = [d for d in range(2 * bit, chips) if d & (2 * bit - 1) == bit]
+        if onward:
+            block = jnp.concatenate([pieces[d] for d in onward], axis=0)
+            block = across(block, "chan", 2 * bit)
+            for i, d in enumerate(onward):
+                rows = slice(i * block_rows, (i + 1) * block_rows)
+                pieces[d ^ bit] = pieces[d ^ bit] + block[rows]
     mine = pieces[0]
-    for d in range(1, chips):
-        mine = mine + across(pieces[d], "chan", 2 * d)
-    receivers = [blocks[0]] + [across(blocks[d], "tm", d) for d in range(1, times)]
+    for bit in bits:
+        mine = mine + across(pieces[bit], "chan", 2 * bit)
+    receivers = [blocks[0]]
+    for d in range(1, times):
+        receivers.append(across(blocks[d], "tm", d))
     receivers = [r.reshape(windows, part, 2 * NF) for r in receivers]
     sources = [mine] + [across(mine, "tm", d) for d in range(1, times)]
 

time: 41.8 us -> 37.4 us (0.89)
  waiting for transfers between devices: 16.5 us -> 12.8 us
  starting transfers between devices: 13.1 us -> 14.2 us
  local copies, waits for them, and re-layouts: 1.05 us -> 0.03 us
  Pallas kernels: 10.6 us -> 9.89 us
    ppermute x10 -> x9, waiting for transfers between devices: 16.5 us -> 12.8 us  [across(): return lax.ppermute(x, axis, [(i, i ^ distance) for i in range(size)])]
    pallas_call x0 -> x1, Pallas kernels: none -> 1.98 us  [shards(): pl.pallas_call(head_kernel, out_shape=[jax.ShapeDtypeStruct((channels, HA...]
    ppermute x10 -> x9, starting transfers between devices: 8.22 us -> 9.76 us  [across(): return lax.ppermute(x, axis, [(i, i ^ distance) for i in range(size)])]
    pallas_call x1, Pallas kernels: 4.11 us -> 2.58 us  [shards(): pl.pallas_call(functools.partial(own_kernel, windows), out_shape=[jax.Sha...]
    pallas_call x2, Pallas kernels: 3.52 us -> 2.32 us  [correlate(): pl.pallas_call(functools.partial(correlate_kernel, windows, factor, count...]
    slice x1 -> x0, local copies, waits for them, and re-layouts: 1.02 us -> none  [shards(): tail = traces[:, samples - HALF - 128:]]
    ppermute x1, starting transfers between devices: 4.89 us -> 4.41 us  [shards(): halo = lax.ppermute(tail, 'tm', [(i - 1, i) for i in range(1, times)])]
  transfers between devices with their start and end apart: 11 -> 10, of which waited for: 7 -> 6; matrix products, arithmetic and copies ran while one was open for 0% -> 0% of each run, Pallas kernels for 12% -> 14%
where the time goes in v4:
time: 37.4 us; the launch traced here: 37.3 us
  starting transfers between devices  14.2 us (38%)
  waiting for transfers between devices  12.8 us (34%)
  Pallas kernels  9.89 us (26%)
    ppermute x9, waiting for transfers between devices, across(): return lax.ppermute(x, axis, [(i, i ^ distance) for i in range(size)])  12.8 us
    ppermute x9, starting transfers between devices, across(): return lax.ppermute(x, axis, [(i, i ^ distance) for i in range(size)])  9.76 us
    ppermute x1, starting transfers between devices, shards(): halo = lax.ppermute(tail, 'tm', [(i - 1, i) for i in range(1, times)])  4.41 us
    pallas_call x1, Pallas kernels, shards(): pl.pallas_call(functools.partial(rest_kernel, shape), out_shape=[jax.Shap...  3 us
    pallas_call x1, Pallas kernels, shards(): pl.pallas_call(functools.partial(own_kernel, windows), out_shape=[jax.Sha...  2.58 us
    pallas_call x2, Pallas kernels, correlate(): pl.pallas_call(functools.partial(correlate_kernel, windows, factor, count...  2.32 us
    pallas_call x1, Pallas kernels, shards(): pl.pallas_call(head_kernel, out_shape=[jax.ShapeDtypeStruct((channels, HA...  1.98 us
  transfers between devices with their start and end apart: 10, of which 6 were waited for; matrix products, arithmetic and copies ran while one was open for 0% of the time, Pallas kernels for 14%

profile of v4, /device:TPU:0, one launch (start us, length us, event | category | flops | bytes accessed | tf_op | source)
XLA Modules:
  0.0 37.3 jit_solution(6509370546114840139)
XLA Ops:
  0.0 0.0 copy-start.2
  0.0 0.5 %collective-permute-start = (s32[1,12]{1,0:T(1,128)}, s32[1,12]{1,0:T(1,128)S(1)}, u32[]{:S(2)}, u32[]{:S(2)}) collective-permute-start(s32[1,12]{1,0:T(1,128)} %param.10), channel_id=1, source_target_pairs={{0,2},{2,0},{4,6},{6,4},{8,10},{10,8},{12,14},{14,12},{1,3},{3,1},... | collective-permute-start | bytes 152 | tf_op jit(solution)/shard_map/ppermute | solution.py:355
  0.5 2.0 %head.1 = (bf16[64,2176]{1,0:T(8,128)(2,1)S(1)}, bf16[64,6144]{1,0:T(8,128)(2,1)S(1)}, f32[33,64]{1,0:T(8,128)S(1)}, bf16[1024,1024]{1,0:T(8,128)(2,1)S(1)}) custom-call(bf16[64,6144]{1,0:T(8,128)(2,1)} %traces_in.1, f32[33,64]{1,0:T(8,128)} %bitcast.8, bf16[1024,1024]{1,0:T(8,128)(2,1)} %constant.10.clone.table_in), custom_call_target="tpu_custom_call" | custom-call | tf_op jit(solution)/shard_map/head/pallas_call | solution.py:365
  2.5 0.0 copy-start
  2.5 0.0 copy-start.1
  2.5 4.4 %collective-permute-start.3 = (bf16[64,2176]{1,0:T(8,128)(2,1)S(1)}, bf16[64,2176]{1,0:T(8,128)(2,1)S(1)}, u32[]{:S(2)}, u32[]{:S(2)}) collective-permute-start(bf16[64,2176]{1,0:T(8,128)(2,1)S(1)} %get-tuple-element.17), channel_id=1, source_target_pairs={{0,1},{2,3},{4,5},{6,7},{8,9},{10,11},{12,13},{14,15},{16,17},{18,... | collective-permute-start | bytes 835592 | tf_op jit(solution)/shard_map/ppermute | solution.py:375
  6.9 0.0 collective-permute-done
  6.9 0.0 copy-done.2
  7.0 1.6 %collective-permute-start.1 = (s32[2,12]{1,0:T(2,128)S(1)}, s32[2,12]{1,0:T(2,128)S(1)}, u32[]{:S(2)}, u32[]{:S(2)}) collective-permute-start(s32[2,12]{1,0:T(2,128)S(1)} %pad_add_fusion.1), channel_id=1, source_target_pairs={{0,4},{2,6},{4,0},{6,2},{8,12},{10,14},{12,8},{14,10},{1,5},{3,7},... | collective-permute-start | bytes 296 | tf_op jit(solution)/shard_map/ppermute | solution.py:355
  8.6 0.1 pad_add_fusion.2.where
  8.7 1.9 %collective-permute-done.1 = s32[2,12]{1,0:T(2,128)S(1)} collective-permute-done((s32[2,12]{1,0:T(2,128)S(1)}, s32[2,12]{1,0:T(2,128)S(1)}, u32[]{:S(2)}, u32[]{:S(2)}) %collective-permute-start.1) | collective-permute-done | bytes 128 | tf_op jit(solution)/shard_map/ppermute | solution.py:355
  10.6 2.7 %collective-permute-start.2 = (s32[4,12]{1,0:T(4,128)S(1)}, s32[4,12]{1,0:T(4,128)S(1)}, u32[]{:S(2)}, u32[]{:S(2)}) collective-permute-start(s32[4,12]{1,0:T(4,128)S(1)} %pad_add_fusion.refs_0_), channel_id=1, source_target_pairs={{0,8},{2,10},{4,12},{6,14},{8,0},{10,2},{12,4},{14,6},{1,9},{3,11}... | collective-permute-start | bytes 584 | tf_op jit(solution)/shard_map/ppermute | solution.py:355
  13.3 2.6 %own.1 = (f32[128,1024]{1,0:T(8,128)S(1)}, bf16[64,1024]{1,0:T(8,128)(2,1)S(1)}, f32[64,1024]{1,0:T(8,128)S(1)}, bf16[64,256]{1,0:T(8,128)(2,1)S(1)}) custom-call(bf16[64,6144]{1,0:T(8,128)(2,1)S(1)} %get-tuple-element.18.traces, f32[33,64]{1,0:T(8,128)S(1)} %get-tuple-element.19.taps.refs_4_, bf16[1024,1024]{1,0:T(8,128)(2,1)S(1)} %get-tuple-element.20.table.refs_5_), custom_call_target="tpu_custom_call" | custom-call | tf_op jit(solution)/shard_map/own/pallas_call | solution.py:384
  15.9 0.0 collective-permute-done.2.refs_1_
  15.9 0.0 collective-permute-done.3.refs_2_
  15.9 0.0 copy-done
  15.9 0.0 copy-done.1
  15.9 3.0 %rest.1 = (bf16[160,1024]{1,0:T(8,128)(2,1)S(1)}, bf16[160,1024]{1,0:T(8,128)(2,1)S(1)}, bf16[96,1024]{1,0:T(8,128)(2,1)S(1)}, bf16[96,1024]{1,0:T(8,128)(2,1)S(1)}) custom-call(s32[2]{0:T(128)S(1)} %pad_add_fusion.2.where, s32[8]{0:T(128)S(1)} %copy-done.1, s32[8,36]{1,0:T(8,128)S(1)} %copy-done, s32[4,12]{1,0:T(4,128)S(1)} %pad_add_fusion.refs_0_, ...), custom_call_target="tpu_custom_call" | custom-call | tf_op jit(solution)/shard_map/rest/pallas_call | solution.py:403
  18.9 0.1 collective-permute-start.5
  19.0 1.6 %collective-permute-done.5 = bf16[160,1024]{1,0:T(8,128)(2,1)S(1)} collective-permute-done((bf16[160,1024]{1,0:T(8,128)(2,1)S(1)}, bf16[160,1024]{1,0:T(8,128)(2,1)S(1)}, u32[]{:S(2)}, u32[]{:S(2)}) %collective-permute-start.5) | collective-permute-done | bytes 327712 | tf_op jit(solution)/shard_map/ppermute | solution.py:355
  20.6 0.1 add.12
  20.7 1.6 %collective-permute-start.7 = (bf16[40,1024]{1,0:T(8,128)(2,1)S(1)}, bf16[40,1024]{1,0:T(8,128)(2,1)S(1)}, u32[]{:S(2)}, u32[]{:S(2)}) collective-permute-start(bf16[40,1024]{1,0:T(8,128)(2,1)S(1)} %get-tuple-element.30), channel_id=1, source_target_pairs={{0,4},{2,6},{4,0},{6,2},{8,12},{10,14},{12,8},{14,10},{1,5},{3,7},... | collective-permute-start | bytes 245768 | tf_op jit(solution)/shard_map/ppermute | solution.py:355
  22.4 0.4 %collective-permute-start.6 = (bf16[40,1024]{1,0:T(8,128)(2,1)S(1)}, bf16[40,1024]{1,0:T(8,128)(2,1)S(1)}, u32[]{:S(2)}, u32[]{:S(2)}) collective-permute-start(bf16[40,1024]{1,0:T(8,128)(2,1)S(1)} %get-tuple-element.29), channel_id=1, source_target_pairs={{0,4},{2,6},{4,0},{6,2},{8,12},{10,14},{12,8},{14,10},{1,5},{3,7},... | collective-permute-start | bytes 245768 | tf_op jit(solution)/shard_map/ppermute | solution.py:355
  22.8 2.9 %collective-permute-done.7 = bf16[40,1024]{1,0:T(8,128)(2,1)S(1)} collective-permute-done((bf16[40,1024]{1,0:T(8,128)(2,1)S(1)}, bf16[40,1024]{1,0:T(8,128)(2,1)S(1)}, u32[]{:S(2)}, u32[]{:S(2)}) %collective-permute-start.7) | collective-permute-done | bytes 81952 | tf_op jit(solution)/shard_map/ppermute | solution.py:355
  25.8 1.9 %collective-permute-start.8 = (bf16[40,1024]{1,0:T(8,128)(2,1)S(1)}, bf16[40,1024]{1,0:T(8,128)(2,1)S(1)}, u32[]{:S(2)}, u32[]{:S(2)}) collective-permute-start(bf16[40,1024]{1,0:T(8,128)(2,1)S(1)} %slice_add_fusion), channel_id=1, source_target_pairs={{0,8},{2,10},{4,12},{6,14},{8,0},{10,2},{12,4},{14,6},{1,9},{3,11}... | collective-permute-start | bytes 245768 | tf_op jit(solution)/shard_map/ppermute | solution.py:355
  27.7 0.8 %collective-permute-start.4 = (bf16[96,1024]{1,0:T(8,128)(2,1)S(1)}, bf16[96,1024]{1,0:T(8,128)(2,1)S(1)}, u32[]{:S(2)}, u32[]{:S(2)}) collective-permute-start(bf16[96,1024]{1,0:T(8,128)(2,1)S(1)} %get-tuple-element.25), channel_id=1, source_target_pairs={{0,1},{1,0},{2,3},{3,2},{4,5},{5,4},{6,7},{7,6},{8,9},{9,8},{10,11... | collective-permute-start | bytes 589832 | tf_op jit(solution)/shard_map/ppermute | solution.py:355
  28.5 0.0 collective-permute-done.6
  28.5 2.7 %collective-permute-done.8 = bf16[40,1024]{1,0:T(8,128)(2,1)S(1)} collective-permute-done((bf16[40,1024]{1,0:T(8,128)(2,1)S(1)}, bf16[40,1024]{1,0:T(8,128)(2,1)S(1)}, u32[]{:S(2)}, u32[]{:S(2)}) %collective-permute-start.8) | collective-permute-done | bytes 81952 | tf_op jit(solution)/shard_map/ppermute | solution.py:355
  31.2 0.1 collective-permute-start.9
  31.3 0.8 %correlate.2.refs_2_ = f32[12,32,1024]{2,1,0:T(8,128)S(1)} custom-call(bf16[3,32,1024]{2,1,0:T(8,128)(2,1)S(1)} %bitcast.6, bf16[40,1024]{1,0:T(8,128)(2,1)S(1)} %fusion.refs_1_), custom_call_target="tpu_custom_call" | custom-call | tf_op jit(solution)/shard_map/correlate/pallas_call | solution.py:331
  32.1 2.2 %collective-permute-done.4 = bf16[96,1024]{1,0:T(8,128)(2,1)S(1)} collective-permute-done((bf16[96,1024]{1,0:T(8,128)(2,1)S(1)}, bf16[96,1024]{1,0:T(8,128)(2,1)S(1)}, u32[]{:S(2)}, u32[]{:S(2)}) %collective-permute-start.4) | collective-permute-done | bytes 196640 | tf_op jit(solution)/shard_map/ppermute | solution.py:355
  34.2 1.4 %collective-permute-done.9.refs_1_ = bf16[40,1024]{1,0:T(8,128)(2,1)S(1)} collective-permute-done((bf16[40,1024]{1,0:T(8,128)(2,1)S(1)}, bf16[40,1024]{1,0:T(8,128)(2,1)S(1)}, u32[]{:S(2)}, u32[]{:S(2)}) %collective-permute-start.9) | collective-permute-done | bytes 81952 | tf_op jit(solution)/shard_map/ppermute | solution.py:355
  35.7 1.6 %correlate.3 = f32[12,32,1024]{2,1,0:T(8,128)} custom-call(bf16[3,32,1024]{2,1,0:T(8,128)(2,1)S(1)} %bitcast.7, bf16[40,1024]{1,0:T(8,128)(2,1)S(1)} %collective-permute-done.9.refs_1_, f32[12,32,1024]{2,1,0:T(8,128)S(1)} %correlate.2.refs_2_), custom_call_target="tpu_custom_call" | custom-call | tf_op jit(solution)/shard_map/correlate/pallas_call | solution.py:331
  (5 shorter events, 0.1 us)
Async XLA Ops:
  0.0 6.9 %copy-start.2 = (s32[1,12]{1,0:T(1,128)S(1)}, s32[1,12]{1,0:T(1,128)}, u32[]{:S(2)}) copy-start(s32[1,12]{1,0:T(1,128)} %param.10) | copy-start | bytes 148
  0.0 6.9 %collective-permute-start = (s32[1,12]{1,0:T(1,128)}, s32[1,12]{1,0:T(1,128)S(1)}, u32[]{:S(2)}, u32[]{:S(2)}) collective-permute-start(s32[1,12]{1,0:T(1,128)} %param.10), channel_id=1, source_target_pairs={{0,2},{2,0},{4,6},{6,4},{8,10},{10,8},{12,14},{14,12},{1,3},{3,1},... | collective-permute-start | bytes 152 | tf_op jit(solution)/shard_map/ppermute | solution.py:355
  2.5 13.4 %copy-start = (s32[8,36]{1,0:T(8,128)S(1)}, s32[8,36]{1,0:T(8,128)}, u32[]{:S(2)}) copy-start(s32[8,36]{1,0:T(8,128)} %slots.1) | copy-start | bytes 3460
  2.5 13.4 %copy-start.1 = (s32[8]{0:T(128)S(1)}, s32[8]{0:T(128)}, u32[]{:S(2)}) copy-start(s32[8]{0:T(128)} %counts.1) | copy-start | bytes 100
  2.5 13.4 %collective-permute-start.3 = (bf16[64,2176]{1,0:T(8,128)(2,1)S(1)}, bf16[64,2176]{1,0:T(8,128)(2,1)S(1)}, u32[]{:S(2)}, u32[]{:S(2)}) collective-permute-start(bf16[64,2176]{1,0:T(8,128)(2,1)S(1)} %get-tuple-element.17), channel_id=1, source_target_pairs={{0,1},{2,3},{4,5},{6,7},{8,9},{10,11},{12,13},{14,15},{16,17},{18,... | collective-permute-start | bytes 835592 | tf_op jit(solution)/shard_map/ppermute | solution.py:375
  7.0 3.6 %collective-permute-start.1 = (s32[2,12]{1,0:T(2,128)S(1)}, s32[2,12]{1,0:T(2,128)S(1)}, u32[]{:S(2)}, u32[]{:S(2)}) collective-permute-start(s32[2,12]{1,0:T(2,128)S(1)} %pad_add_fusion.1), channel_id=1, source_target_pairs={{0,4},{2,6},{4,0},{6,2},{8,12},{10,14},{12,8},{14,10},{1,5},{3,7},... | collective-permute-start | bytes 296 | tf_op jit(solution)/shard_map/ppermute | solution.py:355
  10.6 5.2 %collective-permute-start.2 = (s32[4,12]{1,0:T(4,128)S(1)}, s32[4,12]{1,0:T(4,128)S(1)}, u32[]{:S(2)}, u32[]{:S(2)}) collective-permute-start(s32[4,12]{1,0:T(4,128)S(1)} %pad_add_fusion.refs_0_), channel_id=1, source_target_pairs={{0,8},{2,10},{4,12},{6,14},{8,0},{10,2},{12,4},{14,6},{1,9},{3,11}... | collective-permute-start | bytes 584 | tf_op jit(solution)/shard_map/ppermute | solution.py:355
  18.9 1.7 %collective-permute-start.5 = (bf16[160,1024]{1,0:T(8,128)(2,1)S(1)}, bf16[160,1024]{1,0:T(8,128)(2,1)S(1)}, u32[]{:S(2)}, u32[]{:S(2)}) collective-permute-start(bf16[160,1024]{1,0:T(8,128)(2,1)S(1)} %get-tuple-element.27), channel_id=1, source_target_pairs={{0,2},{2,0},{4,6},{6,4},{8,10},{10,8},{12,14},{14,12},{1,3},{3,1},... | collective-permute-start | bytes 983048 | tf_op jit(solution)/shard_map/ppermute | solution.py:355
  20.7 5.0 %collective-permute-start.7 = (bf16[40,1024]{1,0:T(8,128)(2,1)S(1)}, bf16[40,1024]{1,0:T(8,128)(2,1)S(1)}, u32[]{:S(2)}, u32[]{:S(2)}) collective-permute-start(bf16[40,1024]{1,0:T(8,128)(2,1)S(1)} %get-tuple-element.30), channel_id=1, source_target_pairs={{0,4},{2,6},{4,0},{6,2},{8,12},{10,14},{12,8},{14,10},{1,5},{3,7},... | collective-permute-start | bytes 245768 | tf_op jit(solution)/shard_map/ppermute | solution.py:355
  22.4 6.1 %collective-permute-start.6 = (bf16[40,1024]{1,0:T(8,128)(2,1)S(1)}, bf16[40,1024]{1,0:T(8,128)(2,1)S(1)}, u32[]{:S(2)}, u32[]{:S(2)}) collective-permute-start(bf16[40,1024]{1,0:T(8,128)(2,1)S(1)} %get-tuple-element.29), channel_id=1, source_target_pairs={{0,4},{2,6},{4,0},{6,2},{8,12},{10,14},{12,8},{14,10},{1,5},{3,7},... | collective-permute-start | bytes 245768 | tf_op jit(solution)/shard_map/ppermute | solution.py:355
  25.8 5.4 %collective-permute-start.8 = (bf16[40,1024]{1,0:T(8,128)(2,1)S(1)}, bf16[40,1024]{1,0:T(8,128)(2,1)S(1)}, u32[]{:S(2)}, u32[]{:S(2)}) collective-permute-start(bf16[40,1024]{1,0:T(8,128)(2,1)S(1)} %slice_add_fusion), channel_id=1, source_target_pairs={{0,8},{2,10},{4,12},{6,14},{8,0},{10,2},{12,4},{14,6},{1,9},{3,11}... | collective-permute-start | bytes 245768 | tf_op jit(solution)/shard_map/ppermute | solution.py:355
  27.7 6.5 %collective-permute-start.4 = (bf16[96,1024]{1,0:T(8,128)(2,1)S(1)}, bf16[96,1024]{1,0:T(8,128)(2,1)S(1)}, u32[]{:S(2)}, u32[]{:S(2)}) collective-permute-start(bf16[96,1024]{1,0:T(8,128)(2,1)S(1)} %get-tuple-element.25), channel_id=1, source_target_pairs={{0,1},{1,0},{2,3},{3,2},{4,5},{5,4},{6,7},{7,6},{8,9},{9,8},{10,11... | collective-permute-start | bytes 589832 | tf_op jit(solution)/shard_map/ppermute | solution.py:355
  31.2 4.5 %collective-permute-start.9 = (bf16[40,1024]{1,0:T(8,128)(2,1)S(1)}, bf16[40,1024]{1,0:T(8,128)(2,1)S(1)}, u32[]{:S(2)}, u32[]{:S(2)}) collective-permute-start(bf16[40,1024]{1,0:T(8,128)(2,1)S(1)} %fusion.refs_1_), channel_id=1, source_target_pairs={{0,1},{1,0},{2,3},{3,2},{4,5},{5,4},{6,7},{7,6},{8,9},{9,8},{10,11... | collective-permute-start | bytes 245768 | tf_op jit(solution)/shard_map/ppermute | solution.py:355
